TPU v7x, 32 devices: a whole 2x2x4 slice. The times are simulated.
32 devices in a mesh: grp: 2 (over x), wide: 16 (over z, y, core).
Axes of the slice: x: 2, y: 2, z: 4, core: 2. Of those that a mesh axis runs over, the one named last changes fastest.
Arguments:
- qkv: bfloat16 [4096, 3456], P(('grp', 'wide')), parts along dimension 0, may hold values from -51.854497 to 51.854497
- grid: int32 [4, 2], P('grp'), parts along dimension 0, may hold values from 2 to 512, as said below
- w_out: bfloat16 [1152, 1152], replicated, may hold values from -0.1875 to 0.1875
- ln_gain: float32 [4608], replicated, may hold values from 0.1 to 1.9
- ln_bias: float32 [4608], replicated, may hold values from -3 to 3
- w_merge: bfloat16 [4608, 2048], P('wide'), may hold values from -0.09375 to 0.09375
- w_router: bfloat16 [2048, 8], replicated, may hold values from -0.125 to 0.125
- expert_ids: int32 [1024, 6], P(('grp', 'wide')), parts along dimension 0, may hold values from 0 to 7, as said below
- slot_pos: int32 [1024, 6], P(('grp', 'wide')), parts along dimension 0, may hold values from 0 to 31, as said below
- w_gate: bfloat16 [16, 2048, 704], P('wide'), may hold values from -0.125 to 0.125
- w_up: bfloat16 [16, 2048, 704], P('wide'), may hold values from -0.125 to 0.125
- w_down: bfloat16 [16, 704, 2048], P('wide'), may hold values from -0.15625 to 0.15625
Outputs:
- moe_out: bfloat16 [1024, 2048], P(('grp', 'wide')), parts along dimension 0
There are 2 independent parts, one for each index of `grp`. A program takes and returns all parts, laid end to end along the dimension named above; an argument that names none is the same for every part. Nothing has to cross between parts.
Inputs may be any that keep to these rules, and one draw needn't show every extreme that they name: `expert_ids`: each row names 6 different experts. Among the rows of one device no expert is named more than 32 times, and one expert is named exactly 32 times by the rows of every device. `slot_pos`: among the rows of one device, the pairs naming expert e take the slots 0, 1, ... up to the number of such pairs minus one, each once. `grid`: both numbers are even; one clip's product equals 1024, and every other clip's product lies between 512 and 768.
All inputs are finite; a program needn't handle non-finite values.
Results may differ from a plain program's by a relative error of at most 0.023.
Values may be sent and summed in bfloat16 or wider, within the bound.
A program may use at most 128 MiB of HBM per device.

v0:
```python
import functools

import jax
import jax.numpy as jnp
from jax import lax
from jax.experimental import pallas as pl
from jax.experimental.pallas import tpu as pltpu
from jax.sharding import PartitionSpec as P

HEADS = 16
CLIPS = 2


route_scale = 2.446
norm_eps = 1e-05


def swapped(value, axis, stride):
    mask = 2**stride
    pairs = [(source, source ^ mask) for source in range(lax.axis_size(axis))]
    return lax.ppermute(value, axis, pairs)


def ordered_pair(own_part, partner, upper_bit):
    return jnp.where(
        upper_bit == 1,
        jnp.concatenate([partner, own_part], 0),
        jnp.concatenate([own_part, partner], 0),
    )


def local(
    qkv,
    grid,
    w_out,
    ln_gain,
    ln_bias,
    w_merge,
    w_router,
    expert_ids,
    slot_pos,
    w_gate,
    w_up,
    w_down,
):
    devices = lax.axis_size("wide")
    position_self = lax.axis_index("wide")
    vit_width = w_out.shape[0]
    head_dim = vit_width // HEADS
    groups = devices // HEADS
    local_rows = qkv.shape[0]
    sub_rows = local_rows // groups
    per_clip = devices // CLIPS
    query_send = (
        qkv[:, :vit_width]
        .reshape(groups, sub_rows, HEADS, head_dim)
        .transpose(2, 0, 1, 3)
        .reshape(devices, sub_rows, head_dim)
    )
    key_value = jnp.concatenate(
        [
            qkv[:, vit_width : 2 * vit_width].reshape(local_rows, HEADS, head_dim),
            qkv[:, 2 * vit_width :].reshape(local_rows, HEADS, head_dim),
        ],
        axis=2,
    )
    spread_send = jnp.broadcast_to(
        key_value.transpose(1, 0, 2)[:, None], (HEADS, groups, local_rows, 2 * head_dim)
    ).reshape(devices, local_rows, 2 * head_dim)
    queries, key_rows = (
        lax.all_to_all(query_send, "wide", split_axis=0, concat_axis=0, tiled=True),
        lax.all_to_all(spread_send, "wide", split_axis=0, concat_axis=0, tiled=True),
    )
    key_rows = key_rows[None]
    key_groups = key_rows.shape[0]
    key_count = key_rows.shape[2]
    key_place = (
        jnp.arange(per_clip, dtype=jnp.int32)[None, :, None] * local_rows
        + jnp.arange(key_groups, dtype=jnp.int32)[:, None, None] * local_rows
        + jnp.arange(key_count, dtype=jnp.int32)[None, None, :]
    ).reshape(-1)
    patch_counts = grid[:, 0] * grid[:, 1]
    clip_queries = queries.reshape(CLIPS, per_clip * sub_rows, head_dim)
    query_block_rows = min(512, per_clip * sub_rows)
    score_scale = head_dim ** (-0.5)

    def attend(clip_index):
        key_block = lax.dynamic_slice_in_dim(key_rows, clip_index * per_clip, per_clip, 1).reshape(
            -1, 2 * head_dim
        )
        visible = key_place < lax.dynamic_index_in_dim(patch_counts, clip_index, 0, keepdims=False)
        query_all = lax.dynamic_index_in_dim(clip_queries, clip_index, 0, keepdims=False)

        def one_block(query_block):
            scores = (
                lax.dot_general(
                    query_block,
                    key_block[:, :head_dim],
                    (((1,), (1,)), ((), ())),
                    preferred_element_type=jnp.float32,
                )
                * score_scale
            )
            scores = jnp.where(visible[None, :], scores, -jnp.inf)
            highest = jnp.max(scores, axis=1, keepdims=True)
            weights = jnp.exp(scores - highest)
            running = jnp.sum(weights, axis=1, keepdims=True)
            mixture = jnp.dot(
                weights.astype(jnp.bfloat16),
                key_block[:, head_dim:],
                preferred_element_type=jnp.float32,
            )
            return (mixture / running).astype(jnp.bfloat16)

        return lax.map(one_block, query_all.reshape(-1, query_block_rows, head_dim)).reshape(
            -1, head_dim
        )

    attended = lax.map(attend, jnp.arange(CLIPS, dtype=jnp.int32))
    returned = lax.all_to_all(
        attended.reshape(devices, sub_rows, head_dim),
        "wide",
        split_axis=0,
        concat_axis=0,
        tiled=True,
    )
    attention = (
        returned.reshape(HEADS, groups, sub_rows, head_dim)
        .transpose(1, 2, 0, 3)
        .reshape(local_rows, vit_width)
    )
    projected = jnp.dot(attention, w_out, preferred_element_type=jnp.float32).astype(jnp.bfloat16)
    merged = projected.reshape(local_rows // 4, 4 * vit_width).astype(jnp.float32)
    centre = jnp.mean(merged, axis=1, keepdims=True)
    centered = merged - centre
    spread = jnp.mean(centered * centered, axis=1, keepdims=True)
    normed = (centered * lax.rsqrt(spread + norm_eps) * ln_gain + ln_bias).astype(jnp.bfloat16)
    tok_groups = min(8, devices)
    feat_groups = devices // tok_groups
    merge_rows = w_merge
    for bit_index in range(tok_groups.bit_length() - 1):
        partner = swapped(merge_rows, "wide", bit_index)
        upper_bit = position_self // (1 << bit_index) % 2
        merge_rows = ordered_pair(merge_rows, partner, upper_bit)
    token_count = normed.shape[0]
    part_rows = token_count // tok_groups
    feat_width = normed.shape[1] // feat_groups
    out_width = w_merge.shape[1]
    merge_send = (
        normed.reshape(tok_groups, part_rows, feat_groups, feat_width)
        .transpose(2, 0, 1, 3)
        .reshape(devices, part_rows, feat_width)
    )
    flat_rows = lax.all_to_all(merge_send, "wide", split_axis=0, concat_axis=0, tiled=True).reshape(
        -1, feat_width
    )
    partial_value = jnp.dot(flat_rows, merge_rows, preferred_element_type=jnp.float32).reshape(
        devices, -1, out_width
    )
    summed = lax.all_to_all(partial_value, "wide", split_axis=0, concat_axis=0, tiled=True)
    tokens = (
        jnp.sum(summed.reshape(feat_groups, tok_groups, part_rows, out_width), axis=0)
        .reshape(token_count, out_width)
        .astype(jnp.bfloat16)
    )
    logits = jnp.dot(tokens, w_router, preferred_element_type=jnp.float32)
    experts = w_router.shape[1]
    top_count = expert_ids.shape[1]
    matches = expert_ids[:, :, None] == jnp.arange(experts, dtype=jnp.int32)[None, None, :]
    chosen = jnp.sum(jnp.where(matches, logits[:, None, :], 0.0), axis=2)
    gate_values = jax.nn.sigmoid(chosen)
    route_weight = route_scale * gate_values / jnp.sum(gate_values, axis=1, keepdims=True)
    capacity = min(token_count, 2 * token_count * top_count // experts)
    slot_count = experts * capacity
    target = expert_ids * capacity + slot_pos
    one_hot = jnp.any(
        target[None, :, :] == jnp.arange(slot_count, dtype=jnp.int32)[:, None, None], axis=2
    ).astype(jnp.bfloat16)
    buffer = jnp.dot(one_hot, tokens, preferred_element_type=jnp.float32).astype(jnp.bfloat16)
    gate_half = w_gate[0]
    up_half = w_up[0]
    down_half = w_down[0]
    half_cap = capacity // 2
    dispatch = buffer.reshape(devices, half_cap, out_width)
    portion = lax.all_to_all(dispatch, "wide", split_axis=0, concat_axis=0, tiled=True)
    item_count = portion.shape[1]
    partner_rows = swapped(portion, "wide", 0)
    both_rows = jnp.concatenate([portion, partner_rows], axis=1)
    flat_rows = both_rows.reshape(-1, out_width)
    gate_part = jnp.dot(flat_rows, gate_half, preferred_element_type=jnp.float32)
    up_part = jnp.dot(flat_rows, up_half, preferred_element_type=jnp.float32)
    hidden = (jax.nn.silu(gate_part) * up_part).astype(jnp.bfloat16)
    product = (
        jnp.dot(hidden, down_half, preferred_element_type=jnp.float32)
        .astype(jnp.bfloat16)
        .reshape(devices, 2 * item_count, out_width)
    )
    from_partner = swapped(product[:, item_count:], "wide", 0)
    joined = (
        product[:, :item_count].astype(jnp.float32) + from_partner.astype(jnp.float32)
    ).astype(jnp.bfloat16)
    answers = lax.all_to_all(joined, "wide", split_axis=0, concat_axis=0, tiled=True)
    slot_result = answers.reshape(slot_count, out_width)
    slot_result = lax.optimization_barrier(slot_result)
    picked = jnp.take(slot_result, target.reshape(-1), axis=0).reshape(
        token_count, top_count, out_width
    )
    return jnp.sum(picked.astype(jnp.float32) * route_weight[:, :, None], axis=1).astype(
        jnp.bfloat16
    )


def remote(source, target, send_sem, recv_sem, place):
    return pltpu.make_async_remote_copy(
        src_ref=source,
        dst_ref=target,
        send_sem=send_sem,
        recv_sem=recv_sem,
        device_id={"wide": place},
        device_id_type=pl.DeviceIdType.MESH,
    )


def by_rows(left, right):
    return lax.dot_general(
        left, right, (((1,), (1,)), ((), ())), preferred_element_type=jnp.float32
    )


def greet(places):
    barrier = pltpu.get_barrier_semaphore()
    for place in places:
        pl.semaphore_signal(
            barrier, inc=1, device_id={"wide": place}, device_id_type=pl.DeviceIdType.MESH
        )
    return barrier


def vision_part(
    peers,
    head_dim,
    barrier,
    grid_ref,
    qkv_hbm,
    w_out_hbm,
    gain_ref,
    bias_ref,
    out_ref,
    qkv_ref,
    send,
    recv,
    keys,
    values,
    mixed_send,
    mixed_recv,
    attention,
    mixed,
    w_out_ref,
    send_sem,
    recv_sem,
    back_send_sem,
    back_recv_sem,
    local_sem,
    start_rest,
):
    place = lax.axis_index("wide")
    base = place // peers * peers
    me = place - base
    rows = qkv_ref.shape[0]
    width = w_out_hbm.shape[0]
    heads = HEADS // peers
    span = heads * head_dim
    devices = lax.axis_size("wide")
    qkv_copy = pltpu.make_async_copy(qkv_hbm, qkv_ref, local_sem.at[3])
    qkv_copy.start()
    weight_copy = pltpu.make_async_copy(w_out_hbm, w_out_ref, local_sem.at[0])
    weight_copy.start()
    qkv_copy.wait()
    for peer in range(peers):
        for part in range(3):
            start = part * width + peer * span
            send[peer, :, part * span : (part + 1) * span] = qkv_ref[:, start : start + span]
    pl.semaphore_wait(barrier, devices - 1)
    own = pltpu.make_async_copy(send.at[me], recv.at[me], local_sem.at[1])
    own.start()
    sends = []
    for step in range(1, peers):
        peer = lax.rem(me + step, peers)
        copy = remote(
            send.at[peer], recv.at[me], send_sem.at[peer], recv_sem.at[me], base + peer
        )
        copy.start()
        sends.append(copy)
    start_rest()
    own.wait()
    for step in range(1, peers):
        peer = lax.rem(me + step, peers)
        remote(
            send.at[peer], recv.at[peer], send_sem.at[peer], recv_sem.at[peer], base + peer
        ).wait_recv()
    for head in range(heads):
        low = span + head * head_dim
        keys[head] = recv[:, :, low : low + head_dim].reshape(peers * rows, head_dim)
        low = 2 * span + head * head_dim
        values[head] = recv[:, :, low : low + head_dim].reshape(peers * rows, head_dim)
    factor = head_dim ** (-0.5) * 1.4426950408889634
    clip = place // peers
    count = grid_ref[clip, 0] * grid_ref[clip, 1]
    visible = lax.broadcasted_iota(jnp.int32, (1, peers * rows), 1) < count
    hide = jnp.where(visible, 0.0, -jnp.inf)
    group = 2 if peers % 2 == 0 else 1
    blocks = peers // group

    def one_block(step, carry):
        block = lax.rem(me // group + 1 + step, blocks)
        outcomes = []
        for head in range(heads):
            low = head * head_dim
            query = recv[pl.ds(block * group, group), :, low : low + head_dim].reshape(
                group * rows, head_dim
            )
            scores = lax.dot_general(
                query, keys[head], (((1,), (1,)), ((), ())), preferred_element_type=jnp.float32
            )
            scores = scores + hide
            highest = jnp.max(scores, axis=1, keepdims=True)
            weights = jnp.exp2((scores - highest) * factor)
            running = jnp.sum(weights, axis=1, keepdims=True)
            mixture = jnp.dot(
                weights.astype(jnp.bfloat16), values[head], preferred_element_type=jnp.float32
            )
            outcomes.append((mixture / running).astype(jnp.bfloat16))
        joined = jnp.concatenate([piece.astype(jnp.float32) for piece in outcomes], axis=1)
        for part in range(group):
            peer = block * group + part
            mine = joined[part * rows : (part + 1) * rows]
            mixed_send[peer, :rows, :] = mine[:, :128].astype(jnp.bfloat16)
            tail = jnp.concatenate(
                [mine[:, 128:], jnp.zeros((rows, 256 - span), jnp.float32)], axis=1
            )
            mixed_send[peer, rows:, :] = tail.T[: span - 128].astype(jnp.bfloat16)

            @pl.when(peer != me)
            def _():
                remote(
                    mixed_send.at[peer],
                    mixed_recv.at[me],
                    back_send_sem.at[peer],
                    back_recv_sem.at[me],
                    base + peer,
                ).start()

            @pl.when(peer == me)
            def _():
                pltpu.make_async_copy(
                    mixed_send.at[me], mixed_recv.at[me], local_sem.at[2]
                ).start()

        return carry

    lax.fori_loop(0, blocks, one_block, 0)
    pltpu.make_async_copy(mixed_send.at[me], mixed_recv.at[me], local_sem.at[2]).wait()
    for step in range(1, peers):
        peer = lax.rem(me + step, peers)
        copy = remote(
            mixed_send.at[peer],
            mixed_recv.at[peer],
            back_send_sem.at[peer],
            back_recv_sem.at[peer],
            base + peer,
        )
        copy.wait_recv()
        copy.wait_send()
    for copy in sends:
        copy.wait_send()
    for peer in range(peers):
        start = peer * span
        attention[:, start : start + 128] = mixed_recv[peer, :rows, :]
        tail = mixed_recv[peer, rows:, :].astype(jnp.float32).T
        attention[:, start + 128 : start + span] = tail.astype(jnp.bfloat16)
    weight_copy.wait()
    projected = (
        jnp.dot(attention[...], w_out_ref[...], preferred_element_type=jnp.float32)
        .astype(jnp.bfloat16)
        .astype(jnp.float32)
    )
    tiles = width // 128
    for tile in range(tiles):
        mixed[tile] = projected[:, tile * 128 : (tile + 1) * 128]
    pieces = [
        [mixed[tile, pl.ds(part, rows // 4, stride=4), :] for tile in range(tiles)]
        for part in range(4)
    ]
    total_width = 4 * width
    flat = [piece for row in pieces for piece in row]
    centre = jnp.sum(sum(flat), axis=1, keepdims=True) / total_width
    spread = (
        jnp.sum(sum((piece - centre) * (piece - centre) for piece in flat), axis=1, keepdims=True)
        / total_width
    )
    inverse = lax.rsqrt(spread + norm_eps)
    for index, piece in enumerate(flat):
        out_ref[:, index * 128 : (index + 1) * 128] = (
            (piece - centre) * inverse * gain_ref[index : index + 1, :]
            + bias_ref[index : index + 1, :]
        ).astype(jnp.bfloat16)


def language_part(
    far,
    near,
    run_vision,
    normed_ref,
    ids_ref,
    router_hbm,
    w_merge_hbm,
    w_gate_hbm,
    w_up_hbm,
    w_down_hbm,
    out_ref,
    router_ref,
    merge_rows,
    w_gate,
    w_up,
    w_down,
    norm_send,
    norm_recv,
    part_send,
    y_recv,
    z_send,
    z_recv,
    gathered,
    expert_part,
    core_recv,
    core_sum,
    y2_recv,
    z2_send,
    z2_recv,
    local_sem,
    w_send_sem,
    w_recv_sem,
    n_send_sem,
    n_recv_sem,
    y_send_sem,
    y_recv_sem,
    z_send_sem,
    z_recv_sem,
    g_recv_sem,
    gz_send_sem,
    gy_send_sem,
    gc_send_sem,
    c_send_sem,
    c_recv_sem,
    y2_send_sem,
    y2_recv_sem,
    z2_send_sem,
    z2_recv_sem,
):
    place = lax.axis_index("wide")
    chips = far * near
    core = lax.rem(place, 2)
    chip = place // 2
    a = chip // near
    b = lax.rem(chip, near)
    other = place + 1 - 2 * core
    tokens_here = normed_ref.shape[0]
    depth = w_merge_hbm.shape[0]
    out_width = w_merge_hbm.shape[1]
    experts = chips
    f32 = jnp.float32
    half = jnp.bfloat16

    def at(a_index, b_index, c_index):
        return (a_index * near + b_index) * 2 + c_index

    other_chips = [lax.rem(chip + step, chips) for step in range(1, chips)]
    weight_copies = [
        pltpu.make_async_copy(w_gate_hbm.at[0], w_gate, local_sem.at[0]),
        pltpu.make_async_copy(w_up_hbm.at[0], w_up, local_sem.at[1]),
        pltpu.make_async_copy(w_down_hbm.at[0], w_down, local_sem.at[2]),
    ]
    own_rows = merge_rows.at[pl.ds(core * depth, depth)]
    merge_copy = pltpu.make_async_copy(w_merge_hbm, own_rows, local_sem.at[3])
    merge_swap = remote(w_merge_hbm, own_rows, w_send_sem.at[0], w_recv_sem.at[0], other)

    def start_rest():
        merge_swap.start()
        merge_copy.start()
        for copy in weight_copies:
            copy.start()
        named_rows = router_hbm[...].astype(f32)
        router_ref[...] = jnp.concatenate(
            [
                named_rows,
                named_rows,
                jnp.zeros((router_ref.shape[0] - 2 * experts, out_width), f32),
            ],
            axis=0,
        ).astype(half)

    run_vision(start_rest)
    for q in range(chips):
        norm_send[q] = normed_ref[:, 2 * depth * q : 2 * depth * (q + 1)]
    own_norm = pltpu.make_async_copy(norm_send.at[chip], norm_recv.at[chip], local_sem.at[4])
    own_norm.start()
    for q in other_chips:
        remote(
            norm_send.at[q], norm_recv.at[chip], n_send_sem.at[q], n_recv_sem.at[chip], q * 2 + core
        ).start()
    merge_copy.wait()
    merge_swap.wait_send()
    remote(
        w_merge_hbm,
        merge_rows.at[pl.ds((1 - core) * depth, depth)],
        w_send_sem.at[0],
        w_recv_sem.at[0],
        other,
    ).wait_recv()
    own_norm.wait()
    for q in other_chips:
        copy = remote(
            norm_send.at[q], norm_recv.at[q], n_send_sem.at[q], n_recv_sem.at[q], q * 2 + core
        )
        copy.wait_recv()
        copy.wait_send()
    column_block = min(512, out_width)
    flat = norm_recv[...].reshape(chips * tokens_here, 2 * depth)

    def merge_columns(index, carry):
        columns = pl.ds(pl.multiple_of(index * column_block, column_block), column_block)
        part_send[:, :, columns] = (
            jnp.dot(flat, merge_rows[:, columns], preferred_element_type=f32)
            .astype(half)
            .reshape(chips, tokens_here, column_block)
        )
        return carry

    lax.fori_loop(0, out_width // column_block, merge_columns, 0)

    far_order = [lax.rem(a + step, far) for step in range(1, far)]
    near_order = [lax.rem(b + step, near) for step in range(1, near)]

    def y_copy(a_index, b_index, slot):
        return remote(
            part_send.at[a_index * near + b_index],
            y_recv.at[slot, a_index],
            y_send_sem.at[b_index, a_index],
            y_recv_sem.at[slot, a_index],
            at(a, b_index, core),
        )

    def y_total(a_index):
        total = part_send[a_index * near + b].astype(f32)
        for b_index in near_order:
            y_copy(a_index, b_index, b_index).wait_recv()
            total = total + y_recv[b_index, a_index].astype(f32)
        return total

    def z_copy(a_index, slot):
        return remote(
            z_send.at[a_index],
            z_recv.at[slot],
            z_send_sem.at[a_index],
            z_recv_sem.at[slot],
            at(a_index, b, core),
        )

    for a_index in far_order + [a]:
        for b_index in near_order:
            y_copy(a_index, b_index, b).start()
    for a_index in far_order:
        z_send[a_index] = y_total(a_index).astype(half)
        z_copy(a_index, a).start()
    total = y_total(a)
    for a_index in far_order:
        z_copy(a_index, a_index).wait_recv()
        total = total + z_recv[a_index].astype(f32)
    tokens = total.astype(half)

    lane_count = router_ref.shape[0]
    logits = by_rows(tokens, router_ref[...])
    lane = lax.broadcasted_iota(jnp.int32, (tokens_here, lane_count), 1)
    line = lax.broadcasted_iota(jnp.int32, (lane_count, tokens_here), 0)
    line = jnp.where(line < experts, line, line - experts)
    marks = jnp.zeros((lane_count, tokens_here), f32)
    for k in range(ids_ref.shape[0]):
        marks = jnp.where(line == ids_ref[k : k + 1, :], 1.0, marks)
    same = (
        lax.broadcasted_iota(jnp.int32, (tokens_here, tokens_here), 0)
        == lax.broadcasted_iota(jnp.int32, (tokens_here, tokens_here), 1)
    )
    chosen = by_rows(jnp.where(same, 1.0, 0.0).astype(half), marks.astype(half))
    gates = chosen / (1.0 + jnp.exp(-logits))
    gate_sum = jnp.sum(jnp.where(lane < experts, gates, 0.0), axis=1, keepdims=True)
    route = route_scale * gates / gate_sum
    route_high = route.astype(half)
    route_low = (route - route_high.astype(f32)).astype(half)
    gathered[place, :, :out_width] = tokens
    gathered[place, :, out_width:] = jnp.where(lane < experts, route_high.astype(f32), route_low.astype(f32)).astype(half)

    def share(slot, send_sem, target):
        return remote(gathered.at[slot], gathered.at[slot], send_sem, g_recv_sem.at[slot], target)

    def arrived(slot):
        share(slot, gc_send_sem.at[0], other).wait_recv()

    def to_far(a_index):
        return share(place, gz_send_sem.at[a_index], at(a_index, b, core))

    def to_near(a_index, b_index):
        return share(
            at(a_index, b, core), gy_send_sem.at[a_index, b_index], at(a, b_index, core)
        )

    def to_core(a_index, b_index):
        return share(
            at(a_index, b_index, core), gc_send_sem.at[a_index * near + b_index], other
        )

    def pass_on(a_index):
        for b_index in near_order:
            to_near(a_index, b_index).start()
        to_core(a_index, b).start()

    for a_index in far_order:
        to_far(a_index).start()
    pass_on(a)
    for copy in weight_copies:
        copy.wait()

    def core_copy(a_index, b_index, c_index):
        return remote(
            expert_part.at[at(a_index, b_index, c_index)],
            core_recv.at[a_index * near + b_index],
            c_send_sem.at[a_index * near + b_index],
            c_recv_sem.at[a_index * near + b_index],
            other,
        )

    def y2_copy(a_index, b_index, slot):
        return remote(
            core_sum.at[a_index * near + b_index],
            y2_recv.at[slot, a_index],
            y2_send_sem.at[b_index, a_index],
            y2_recv_sem.at[slot, a_index],
            at(a, b_index, core),
        )

    def z2_copy(a_index, slot):
        return remote(
            z2_send.at[a_index],
            z2_recv.at[slot],
            z2_send_sem.at[a_index],
            z2_recv_sem.at[slot],
            at(a_index, b, core),
        )

    chunk = near * 2
    expert = place // 2
    column_blocks = out_width // column_block

    def run_chunk(step):
        a_index = lax.rem(a + step, far)
        for b_index in near_order:
            arrived(at(a_index, b_index, core))
            to_core(a_index, b_index).start()
        for b_index in range(near):
            arrived(at(a_index, b_index, 1 - core))
        slots = pl.ds(a_index * chunk, chunk)
        rows = gathered[slots, :, :out_width].reshape(chunk * tokens_here, out_width)
        table = gathered[slots, :, out_width:].reshape(chunk * tokens_here, lane_count).astype(f32)
        table_lane = lax.broadcasted_iota(jnp.int32, table.shape, 1)
        mine = jnp.logical_or(table_lane == expert, table_lane == expert + experts)
        scale = jnp.sum(jnp.where(mine, table, 0.0), axis=1, keepdims=True)
        gate_part = by_rows(rows, w_gate[...])
        up_part = by_rows(rows, w_up[...])
        hidden = (gate_part / (1.0 + jnp.exp(-gate_part)) * up_part).astype(half)
        for index in range(column_blocks):
            columns = pl.ds(index * column_block, column_block)
            product = jnp.dot(hidden, w_down[:, columns], preferred_element_type=f32).astype(half)
            expert_part[slots, :, columns] = (
                (product.astype(f32) * scale)
                .astype(half)
                .reshape(chunk, tokens_here, column_block)
            )
        for b_index in range(near):
            core_copy(a_index, b_index, 1 - core).start()

    def join_cores(step):
        a_index = lax.rem(a + step, far)
        for b_index in near_order + [b]:
            core_copy(a_index, b_index, 1 - core).wait_recv()
            core_sum[a_index * near + b_index] = (
                expert_part[at(a_index, b_index, core)].astype(f32)
                + core_recv[a_index * near + b_index].astype(f32)
            ).astype(half)
        for b_index in near_order:
            y2_copy(a_index, b_index, b).start()

    def y2_total(a_index):
        value = core_sum[a_index * near + b].astype(f32)
        for b_index in near_order:
            y2_copy(a_index, b_index, b_index).wait_recv()
            value = value + y2_recv[b_index, a_index].astype(f32)
        return value

    def join_near(step):
        a_index = lax.rem(a + step, far)
        z2_send[a_index] = y2_total(a_index).astype(half)
        z2_copy(a_index, a).start()

    def chunks(step, carry):
        @pl.when(step == 0)
        def _():
            for a_index in far_order:
                arrived(at(a_index, b, core))
                pass_on(a_index)

        @pl.when(step >= 1)
        def _():
            join_cores(step - 1)

        @pl.when(step >= 3)
        def _():
            join_near(step - 2)

        run_chunk(step)
        return carry

    lax.fori_loop(0, far, chunks, 0)
    join_cores(far - 1)
    for step in range(max(1, far - 2), far):
        join_near(step)
    value = y2_total(a)
    for a_index in far_order:
        z2_copy(a_index, a_index).wait_recv()
        value = value + z2_recv[a_index].astype(f32)
    out_ref[...] = value.astype(half)

    for a_index in far_order:
        z_copy(a_index, a).wait_send()
        to_far(a_index).wait_send()
        z2_copy(a_index, a).wait_send()
    for a_index in far_order + [a]:
        for b_index in near_order:
            y_copy(a_index, b_index, b).wait_send()
            to_near(a_index, b_index).wait_send()
            y2_copy(a_index, b_index, b).wait_send()
        for b_index in near_order + [b]:
            to_core(a_index, b_index).wait_send()
            core_copy(a_index, b_index, 1 - core).wait_send()


def layer_kernel(far, near, peers, head_dim, *refs):
    operands, out_ref, normed = refs[:11], refs[11], refs[12]
    grid_ref, qkv_hbm, w_out_hbm, gain_ref, bias_ref = operands[:5]
    scratch = refs[13:]
    vision_scratch, language_scratch = scratch[:15], scratch[15:]
    place = lax.axis_index("wide")
    devices = lax.axis_size("wide")
    barrier = greet([lax.rem(place + step, devices) for step in range(1, devices)])

    def run_vision(start_rest):
        vision_part(
            peers,
            head_dim,
            barrier,
            grid_ref,
            qkv_hbm,
            w_out_hbm,
            gain_ref,
            bias_ref,
            normed,
            *vision_scratch,
            start_rest,
        )

    language_part(far, near, run_vision, normed, *operands[5:], out_ref, *language_scratch)


def fast_local(
    qkv,
    grid,
    w_out,
    ln_gain,
    ln_bias,
    w_merge,
    w_router,
    expert_ids,
    slot_pos,
    w_gate,
    w_up,
    w_down,
):
    devices = lax.axis_size("wide")
    peers = devices // CLIPS
    patch_rows = qkv.shape[0]
    width = w_out.shape[0]
    head_dim = width // HEADS
    heads = HEADS // peers
    span = heads * head_dim
    chips = devices // 2
    near = 1
    while 4 * near * near <= chips:
        near *= 2
    far = chips // near
    rows = patch_rows // 4
    depth, out_width = w_merge.shape
    experts = w_router.shape[1]
    lanes = -(-2 * experts // 128) * 128
    hidden = w_gate.shape[2]
    whole = pl.BlockSpec(memory_space=pltpu.VMEM)
    away = pl.BlockSpec(memory_space=pl.ANY)
    half = jnp.bfloat16
    block = (rows, out_width)
    dma = pltpu.SemaphoreType.DMA
    return pl.pallas_call(
        functools.partial(layer_kernel, far, near, peers, head_dim),
        out_shape=jax.ShapeDtypeStruct(block, half),
        in_specs=[
            pl.BlockSpec(memory_space=pltpu.SMEM),
            away,
            away,
            whole,
            whole,
            whole,
            whole,
            away,
            away,
            away,
            away,
        ],
        out_specs=whole,
        scratch_shapes=[
            pltpu.VMEM((rows, 4 * width), half),
            pltpu.VMEM((patch_rows, 3 * width), half),
            pltpu.VMEM((peers, patch_rows, 3 * span), half),
            pltpu.VMEM((peers, patch_rows, 3 * span), half),
            pltpu.VMEM((heads, peers * patch_rows, head_dim), half),
            pltpu.VMEM((heads, peers * patch_rows, head_dim), half),
            pltpu.VMEM((peers, patch_rows + span - 128, 128), half),
            pltpu.VMEM((peers, patch_rows + span - 128, 128), half),
            pltpu.VMEM((patch_rows, width), half),
            pltpu.VMEM((width // 128, patch_rows, 128), jnp.float32),
            pltpu.VMEM((width, width), half),
            dma((peers,)),
            dma((peers,)),
            dma((peers,)),
            dma((peers,)),
            dma((4,)),
            pltpu.VMEM((lanes, out_width), half),
            pltpu.VMEM((2 * depth, out_width), half),
            pltpu.VMEM((hidden, out_width), half),
            pltpu.VMEM((hidden, out_width), half),
            pltpu.VMEM((hidden, out_width), half),
            pltpu.VMEM((chips, rows, 2 * depth), half),
            pltpu.VMEM((chips, rows, 2 * depth), half),
            pltpu.VMEM((chips, *block), half),
            pltpu.VMEM((near, far, *block), half),
            pltpu.VMEM((far, *block), half),
            pltpu.VMEM((far, *block), half),
            pltpu.VMEM((devices, rows, out_width + lanes), half),
            pltpu.VMEM((devices, *block), half),
            pltpu.VMEM((chips, *block), half),
            pltpu.VMEM((chips, *block), half),
            pltpu.VMEM((near, far, *block), half),
            pltpu.VMEM((far, *block), half),
            pltpu.VMEM((far, *block), half),
            dma((5,)),
            dma((1,)),
            dma((1,)),
            dma((chips,)),
            dma((chips,)),
            dma((near, far)),
            dma((near, far)),
            dma((far,)),
            dma((far,)),
            dma((devices,)),
            dma((far,)),
            dma((far, near)),
            dma((chips,)),
            dma((chips,)),
            dma((chips,)),
            dma((near, far)),
            dma((near, far)),
            dma((far,)),
            dma((far,)),
        ],
        compiler_params=pltpu.CompilerParams(
            collective_id=0, has_side_effects=True, vmem_limit_bytes=62 * 2**20
        ),
        name="layer",
    )(
        grid,
        qkv,
        w_out,
        ln_gain.reshape(-1, 128),
        ln_bias.reshape(-1, 128),
        expert_ids.T,
        w_router.T,
        w_merge,
        w_gate.swapaxes(1, 2),
        w_up.swapaxes(1, 2),
        w_down,
    )


def either(*operands):
    devices = lax.axis_size("wide")
    qkv, w_router, expert_ids = operands[0], operands[6], operands[7]
    token_count = qkv.shape[0] // 4
    experts = w_router.shape[1]
    dense = 2 * token_count * expert_ids.shape[1] >= experts * token_count
    whole_heads = HEADS % (devices // CLIPS) == 0 and devices == 2 * experts
    if not (dense and whole_heads):
        return local(*operands)
    span = HEADS // (devices // CLIPS) * (operands[2].shape[0] // HEADS)
    packs = qkv.shape[0] == 128 and 128 < span < 256 and span % 16 == 0
    return fast_local(*operands) if packs else local(*operands)


def solution(mesh):
    placed = (
        P(("grp", "wide"), None),
        P("grp", None),
        P(),
        P(),
        P(),
        P("wide", None),
        P(),
        P(("grp", "wide"), None),
        P(("grp", "wide"), None),
        P("wide", None, None),
        P("wide", None, None),
        P("wide", None, None),
    )
    return jax.shard_map(
        either, mesh=mesh, in_specs=placed, out_specs=P(("grp", "wide"), None), check_vma=False
    )
```

profile of v0, /device:TPU:0, one launch (start us, length us, event | category | flops | bytes accessed | tf_op | source)
XLA Modules:
  0.0 99.5 jit_solution(16537031701260908071)
XLA Ops:
  0.0 97.9 %layer.1 = bf16[32,2048]{1,0:T(8,128)(2,1)} custom-call(s32[2,2]{1,0:T(2,128)} %refs_0_.1, bf16[128,3456]{1,0:T(8,128)(2,1)} %refs_1_.1, bf16[1152,1152]{1,0:T(8,128)(2,1)} %refs_2_.1, f32[36,128]{1,0:T(8,128)} %bitcast.9, f32[36,128]{1,0:T(8,128)} %bitcast.10, s32[6,32]{1,0:T(8,128)} %bitcast.11, bf16[8,2048]{1,0:T(8,128)(2,1)} %bitcast.8, ...), custom_call_target="tpu_custom_call" | custom-call | tf_op jit(solution)/shard_map/layer/pallas_call | solution.py:817
  97.9 1.6 %copy.13 = bf16[32,2048]{1,0:T(8,128)(2,1)} copy(bf16[32,2048]{1,0:T(8,128)(2,1)} %layer.1) | data formatting | bytes 262144
where the time goes:
time: 99.7 us; the launch traced here: 99.5 us
  Pallas kernels  97.9 us (98%)
  local copies, waits for them, and re-layouts  1.57 us (2%)
    pallas_call x1, Pallas kernels, fast_local(): pl.pallas_call(functools.partial(layer_kernel, far, near, peers, head_dim...  97.9 us

commit v1 on v0

--- a/solution.py
+++ b/solution.py
@@ -429,7 +429,9 @@
     y_recv,
     z_send,
     z_recv,
+    token_sum,
     gathered,
+    hidden_rows,
     expert_part,
     core_recv,
     core_sum,
@@ -537,45 +539,90 @@
 
     lax.fori_loop(0, out_width // column_block, merge_columns, 0)
 
-    far_order = [lax.rem(a + step, far) for step in range(1, far)]
     near_order = [lax.rem(b + step, near) for step in range(1, near)]
-
-    def y_copy(a_index, b_index, slot):
+    pieces = out_width // column_block
+    flip = a // (far // 2)
+    mirrored = a + flip * (far - 1 - 2 * a)
+
+    def columns_of(piece):
+        return pl.ds(piece * column_block, column_block)
+
+    def far_first(step):
+        value = far - 1 - step
+        value = value - (mirrored - value + far) // far
+        return value + flip * (far - 1 - 2 * value)
+
+    def y_copy(a_index, b_index, slot, piece):
+        columns = columns_of(piece)
         return remote(
-            part_send.at[a_index * near + b_index],
-            y_recv.at[slot, a_index],
-            y_send_sem.at[b_index, a_index],
-            y_recv_sem.at[slot, a_index],
+            part_send.at[a_index * near + b_index, :, columns],
+            y_recv.at[slot, a_index, :, columns],
+            y_send_sem.at[b_index, a_index, piece],
+            y_recv_sem.at[slot, a_index, piece],
             at(a, b_index, core),
         )
 
-    def y_total(a_index):
-        total = part_send[a_index * near + b].astype(f32)
+    def y_total(a_index, piece):
+        columns = columns_of(piece)
+        value = part_send[a_index * near + b, :, columns].astype(f32)
         for b_index in near_order:
-            y_copy(a_index, b_index, b_index).wait_recv()
-            total = total + y_recv[b_index, a_index].astype(f32)
-        return total
-
-    def z_copy(a_index, slot):
+            y_copy(a_index, b_index, b_index, piece).wait_recv()
+            value = value + y_recv[b_index, a_index, :, columns].astype(f32)
+        return value
+
+    def z_copy(a_index, rightward, target, piece):
+        columns = columns_of(piece)
         return remote(
-            z_send.at[a_index],
-            z_recv.at[slot],
-            z_send_sem.at[a_index],
-            z_recv_sem.at[slot],
-            at(a_index, b, core),
-        )
-
-    for a_index in far_order + [a]:
-        for b_index in near_order:
-            y_copy(a_index, b_index, b).start()
-    for a_index in far_order:
-        z_send[a_index] = y_total(a_index).astype(half)
-        z_copy(a_index, a).start()
-    total = y_total(a)
-    for a_index in far_order:
-        z_copy(a_index, a_index).wait_recv()
-        total = total + z_recv[a_index].astype(f32)
-    tokens = total.astype(half)
+            z_send.at[a_index, :, columns],
+            z_recv.at[rightward, a_index, :, columns],
+            z_send_sem.at[a_index, piece],
+            z_recv_sem.at[rightward, a_index, piece],
+            at(target, b, core),
+        )
+
+    far_targets = [far_first(step) for step in range(far - 1)]
+    for a_index in far_targets + [a]:
+        for piece in range(pieces):
+            for b_index in near_order:
+                y_copy(a_index, b_index, b, piece).start()
+    z_sends = []
+    for a_index in far_targets:
+        rightward = (a_index - a + far) // far
+        following = a + 2 * rightward - 1
+        behind = rightward * a + (1 - rightward) * (far - 1 - a)
+        for piece in range(pieces):
+            columns = columns_of(piece)
+            value = y_total(a_index, piece)
+            copy = z_copy(a_index, rightward, following, piece)
+            z_sends.append(copy)
+
+            @pl.when(behind == 0)
+            def _():
+                z_send[a_index, :, columns] = value.astype(half)
+
+            @pl.when(behind > 0)
+            def _():
+                copy.wait_recv()
+                z_send[a_index, :, columns] = (
+                    value + z_recv[rightward, a_index, :, columns].astype(f32)
+                ).astype(half)
+
+            copy.start()
+    for piece in range(pieces):
+        columns = columns_of(piece)
+        token_sum[:, columns] = y_total(a, piece)
+
+        @pl.when(a > 0)
+        def _():
+            z_copy(a, 1, a, piece).wait_recv()
+            token_sum[:, columns] = token_sum[:, columns] + z_recv[1, a, :, columns].astype(f32)
+
+        @pl.when(a < far - 1)
+        def _():
+            z_copy(a, 0, a, piece).wait_recv()
+            token_sum[:, columns] = token_sum[:, columns] + z_recv[0, a, :, columns].astype(f32)
+
+    tokens = token_sum[...].astype(half)
 
     lane_count = router_ref.shape[0]
     logits = by_rows(tokens, router_ref[...])
@@ -622,45 +669,87 @@
             to_near(a_index, b_index).start()
         to_core(a_index, b).start()
 
-    for a_index in far_order:
-        to_far(a_index).start()
+    def paired(step):
+        value, bit = 0, 1
+        while bit < far:
+            mine, theirs = a // bit % 2, step // bit % 2
+            value = value + bit * (mine + theirs - 2 * mine * theirs)
+            bit *= 2
+        return value
+
     pass_on(a)
+    for step in range(1, far):
+        to_far(paired(step)).start()
     for copy in weight_copies:
         copy.wait()
 
-    def core_copy(a_index, b_index, c_index):
+    def core_copy(a_index, side, piece):
+        columns = columns_of(piece)
         return remote(
-            expert_part.at[at(a_index, b_index, c_index)],
-            core_recv.at[a_index * near + b_index],
-            c_send_sem.at[a_index * near + b_index],
-            c_recv_sem.at[a_index * near + b_index],
+            expert_part.at[a_index, side, :, :, columns],
+            core_recv.at[a_index, :, :, columns],
+            c_send_sem.at[a_index, piece],
+            c_recv_sem.at[a_index, piece],
             other,
         )
 
-    def y2_copy(a_index, b_index, slot):
+    def y2_copy(a_index, b_index, slot, piece):
+        columns = columns_of(piece)
         return remote(
-            core_sum.at[a_index * near + b_index],
-            y2_recv.at[slot, a_index],
-            y2_send_sem.at[b_index, a_index],
-            y2_recv_sem.at[slot, a_index],
+            core_sum.at[a_index, b_index, :, columns],
+            y2_recv.at[slot, a_index, :, columns],
+            y2_send_sem.at[b_index, a_index, piece],
+            y2_recv_sem.at[slot, a_index, piece],
             at(a, b_index, core),
         )
 
-    def z2_copy(a_index, slot):
+    def z2_copy(a_index, slot, piece):
+        columns = columns_of(piece)
         return remote(
-            z2_send.at[a_index],
-            z2_recv.at[slot],
-            z2_send_sem.at[a_index],
-            z2_recv_sem.at[slot],
+            z2_send.at[a_index, :, columns],
+            z2_recv.at[slot, :, columns],
+            z2_send_sem.at[a_index, piece],
+            z2_recv_sem.at[slot, piece],
             at(a_index, b, core),
         )
 
     chunk = near * 2
     expert = place // 2
-    column_blocks = out_width // column_block
-
-    def run_chunk(step):
-        a_index = lax.rem(a + step, far)
+
+    def y2_start(a_index, piece):
+        for b_index in near_order:
+            y2_copy(a_index, b_index, b, piece).start()
+
+    def join_cores(a_index, piece):
+        columns = columns_of(piece)
+        core_copy(a_index, 1 - core, piece).wait_recv()
+        core_sum[a_index, :, :, columns] = (
+            expert_part[a_index, core, :, :, columns].astype(f32)
+            + core_recv[a_index, :, :, columns].astype(f32)
+        ).astype(half)
+
+    def y2_total(a_index, piece):
+        columns = columns_of(piece)
+        value = core_sum[a_index, b, :, columns].astype(f32)
+        for b_index in near_order:
+            y2_copy(a_index, b_index, b_index, piece).wait_recv()
+            value = value + y2_recv[b_index, a_index, :, columns].astype(f32)
+        return value
+
+    def join_near(a_index):
+        for piece in range(pieces):
+            z2_send[a_index, :, columns_of(piece)] = y2_total(a_index, piece).astype(half)
+            z2_copy(a_index, a, piece).start()
+
+    def chunks(step, carry):
+        a_index = paired(step)
+
+        @pl.when(step < far - 1)
+        def _():
+            upcoming = paired(step + 1)
+            arrived(at(upcoming, b, core))
+            pass_on(upcoming)
+
         for b_index in near_order:
             arrived(at(a_index, b_index, core))
             to_core(a_index, b_index).start()
@@ -674,81 +763,72 @@
         scale = jnp.sum(jnp.where(mine, table, 0.0), axis=1, keepdims=True)
         gate_part = by_rows(rows, w_gate[...])
         up_part = by_rows(rows, w_up[...])
-        hidden = (gate_part / (1.0 + jnp.exp(-gate_part)) * up_part).astype(half)
-        for index in range(column_blocks):
-            columns = pl.ds(index * column_block, column_block)
+        hidden_rows[...] = (gate_part / (1.0 + jnp.exp(-gate_part)) * up_part).astype(half)
+
+        @pl.when(step == 1)
+        def _():
+            for piece in range(pieces):
+                join_cores(a, piece)
+
+        @pl.when(step > 1)
+        def _():
+            previous = paired(step - 1)
+            for piece in range(pieces):
+                join_cores(previous, piece)
+                y2_start(previous, piece)
+
+        hidden = hidden_rows[...]
+        for piece in range(pieces):
+            columns = columns_of(piece)
             product = jnp.dot(hidden, w_down[:, columns], preferred_element_type=f32).astype(half)
-            expert_part[slots, :, columns] = (
-                (product.astype(f32) * scale)
-                .astype(half)
-                .reshape(chunk, tokens_here, column_block)
-            )
+            scaled = (product.astype(f32) * scale).astype(half)
+            for b_index in range(near):
+                for side in range(2):
+                    start = (b_index * 2 + side) * tokens_here
+                    expert_part[a_index, side, b_index, :, columns] = scaled[
+                        start : start + tokens_here
+                    ]
+            core_copy(a_index, 1 - core, piece).start()
+
+        @pl.when(step > 2)
+        def _():
+            join_near(paired(step - 2))
+
+        return carry
+
+    lax.fori_loop(0, far, chunks, 0)
+    final = paired(far - 1)
+    for piece in range(pieces):
+        join_cores(final, piece)
+        y2_start(final, piece)
+    for piece in range(pieces):
+        y2_start(a, piece)
+    for step in range(max(1, far - 2), far):
+        join_near(paired(step))
+    for piece in range(pieces):
+        columns = columns_of(piece)
+        value = y2_total(a, piece)
+        for step in range(1, far):
+            z2_copy(paired(step), paired(step), piece).wait_recv()
+            value = value + z2_recv[paired(step), :, columns].astype(f32)
+        out_ref[:, columns] = value.astype(half)
+
+    for copy in z_sends:
+        copy.wait_send()
+    for step in range(1, far):
+        to_far(paired(step)).wait_send()
+        for piece in range(pieces):
+            z2_copy(paired(step), a, piece).wait_send()
+    for a_index in range(far):
+        for piece in range(pieces):
+            core_copy(a_index, 1 - core, piece).wait_send()
         for b_index in range(near):
-            core_copy(a_index, b_index, 1 - core).start()
-
-    def join_cores(step):
-        a_index = lax.rem(a + step, far)
-        for b_index in near_order + [b]:
-            core_copy(a_index, b_index, 1 - core).wait_recv()
-            core_sum[a_index * near + b_index] = (
-                expert_part[at(a_index, b_index, core)].astype(f32)
-                + core_recv[a_index * near + b_index].astype(f32)
-            ).astype(half)
+            to_core(a_index, b_index).wait_send()
         for b_index in near_order:
-            y2_copy(a_index, b_index, b).start()
-
-    def y2_total(a_index):
-        value = core_sum[a_index * near + b].astype(f32)
-        for b_index in near_order:
-            y2_copy(a_index, b_index, b_index).wait_recv()
-            value = value + y2_recv[b_index, a_index].astype(f32)
-        return value
-
-    def join_near(step):
-        a_index = lax.rem(a + step, far)
-        z2_send[a_index] = y2_total(a_index).astype(half)
-        z2_copy(a_index, a).start()
-
-    def chunks(step, carry):
-        @pl.when(step == 0)
-        def _():
-            for a_index in far_order:
-                arrived(at(a_index, b, core))
-                pass_on(a_index)
-
-        @pl.when(step >= 1)
-        def _():
-            join_cores(step - 1)
-
-        @pl.when(step >= 3)
-        def _():
-            join_near(step - 2)
-
-        run_chunk(step)
-        return carry
-
-    lax.fori_loop(0, far, chunks, 0)
-    join_cores(far - 1)
-    for step in range(max(1, far - 2), far):
-        join_near(step)
-    value = y2_total(a)
-    for a_index in far_order:
-        z2_copy(a_index, a_index).wait_recv()
-        value = value + z2_recv[a_index].astype(f32)
-    out_ref[...] = value.astype(half)
-
-    for a_index in far_order:
-        z_copy(a_index, a).wait_send()
-        to_far(a_index).wait_send()
-        z2_copy(a_index, a).wait_send()
-    for a_index in far_order + [a]:
-        for b_index in near_order:
-            y_copy(a_index, b_index, b).wait_send()
             to_near(a_index, b_index).wait_send()
-            y2_copy(a_index, b_index, b).wait_send()
-        for b_index in near_order + [b]:
-            to_core(a_index, b_index).wait_send()
-            core_copy(a_index, b_index, 1 - core).wait_send()
+            for piece in range(pieces):
+                y_copy(a_index, b_index, b, piece).wait_send()
+                y2_copy(a_index, b_index, b, piece).wait_send()
 
 
 def layer_kernel(far, near, peers, head_dim, *refs):
@@ -814,6 +894,7 @@
     half = jnp.bfloat16
     block = (rows, out_width)
     dma = pltpu.SemaphoreType.DMA
+    pieces = out_width // min(512, out_width)
     return pl.pallas_call(
         functools.partial(layer_kernel, far, near, peers, head_dim),
         out_shape=jax.ShapeDtypeStruct(block, half),
@@ -858,11 +939,13 @@
             pltpu.VMEM((chips, *block), half),
             pltpu.VMEM((near, far, *block), half),
             pltpu.VMEM((far, *block), half),
-            pltpu.VMEM((far, *block), half),
+            pltpu.VMEM((2, far, *block), half),
+            pltpu.VMEM(block, jnp.float32),
             pltpu.VMEM((devices, rows, out_width + lanes), half),
-            pltpu.VMEM((devices, *block), half),
-            pltpu.VMEM((chips, *block), half),
-            pltpu.VMEM((chips, *block), half),
+            pltpu.VMEM((2 * near * rows, hidden), half),
+            pltpu.VMEM((far, 2, near, *block), half),
+            pltpu.VMEM((far, near, *block), half),
+            pltpu.VMEM((far, near, *block), half),
             pltpu.VMEM((near, far, *block), half),
             pltpu.VMEM((far, *block), half),
             pltpu.VMEM((far, *block), half),
@@ -871,20 +954,20 @@
             dma((1,)),
             dma((chips,)),
             dma((chips,)),
-            dma((near, far)),
-            dma((near, far)),
-            dma((far,)),
-            dma((far,)),
+            dma((near, far, pieces)),
+            dma((near, far, pieces)),
+            dma((far, pieces)),
+            dma((2, far, pieces)),
             dma((devices,)),
             dma((far,)),
             dma((far, near)),
             dma((chips,)),
-            dma((chips,)),
-            dma((chips,)),
-            dma((near, far)),
-            dma((near, far)),
-            dma((far,)),
-            dma((far,)),
+            dma((far, pieces)),
+            dma((far, pieces)),
+            dma((near, far, pieces)),
+            dma((near, far, pieces)),
+            dma((far, pieces)),
+            dma((far, pieces)),
         ],
         compiler_params=pltpu.CompilerParams(
             collective_id=0, has_side_effects=True, vmem_limit_bytes=62 * 2**20

time: 99.7 us -> 100 us (level)
  no operation moved by 1% of the time
where the time goes in v1:
time: 100 us; the launch traced here: 99.6 us
  Pallas kernels  98 us (98%)
  local copies, waits for them, and re-layouts  1.57 us (2%)
    pallas_call x1, Pallas kernels, fast_local(): pl.pallas_call(functools.partial(layer_kernel, far, near, peers, head_dim...  98 us

profile of v1, /device:TPU:0, one launch (start us, length us, event | category | flops | bytes accessed | tf_op | source)
XLA Modules:
  0.0 99.6 jit_solution(18109155552148068229)
XLA Ops:
  0.0 98.0 %layer.1 = bf16[32,2048]{1,0:T(8,128)(2,1)} custom-call(s32[2,2]{1,0:T(2,128)} %refs_0_.1, bf16[128,3456]{1,0:T(8,128)(2,1)} %refs_1_.1, bf16[1152,1152]{1,0:T(8,128)(2,1)} %refs_2_.1, f32[36,128]{1,0:T(8,128)} %bitcast.9, f32[36,128]{1,0:T(8,128)} %bitcast.10, s32[6,32]{1,0:T(8,128)} %bitcast.11, bf16[8,2048]{1,0:T(8,128)(2,1)} %bitcast.8, ...), custom_call_target="tpu_custom_call" | custom-call | tf_op jit(solution)/shard_map/layer/pallas_call | solution.py:898
  98.0 1.6 %copy.13 = bf16[32,2048]{1,0:T(8,128)(2,1)} copy(bf16[32,2048]{1,0:T(8,128)(2,1)} %layer.1) | data formatting | bytes 262144

commit v2 on v1

--- a/solution.py
+++ b/solution.py
@@ -13,6 +13,7 @@
 
 route_scale = 2.446
 norm_eps = 1e-05
+column_parts = 2
 
 
 def swapped(value, axis, stride):
@@ -429,7 +430,6 @@
     y_recv,
     z_send,
     z_recv,
-    token_sum,
     gathered,
     hidden_rows,
     expert_part,
@@ -539,92 +539,128 @@
 
     lax.fori_loop(0, out_width // column_block, merge_columns, 0)
 
-    near_order = [lax.rem(b + step, near) for step in range(1, near)]
+    near_steps = range(1, near)
     pieces = out_width // column_block
-    flip = a // (far // 2)
-    mirrored = a + flip * (far - 1 - 2 * a)
+    parts = column_parts
+    part_width = out_width // parts
 
     def columns_of(piece):
         return pl.ds(piece * column_block, column_block)
 
-    def far_first(step):
-        value = far - 1 - step
-        value = value - (mirrored - value + far) // far
-        return value + flip * (far - 1 - 2 * value)
-
-    def y_copy(a_index, b_index, slot, piece):
-        columns = columns_of(piece)
+    def part_of(part):
+        return pl.ds(part * part_width, part_width)
+
+    def paired(step):
+        value, bit = 0, 1
+        while bit < far:
+            mine, theirs = a // bit % 2, step // bit % 2
+            value = value + bit * (mine + theirs - 2 * mine * theirs)
+            bit *= 2
+        return value
+
+    def y_copy(a_index, step, slot, part):
+        target = lax.rem(b + step, near)
+        columns = part_of(part)
         return remote(
-            part_send.at[a_index * near + b_index, :, columns],
+            part_send.at[a_index * near + target, :, columns],
             y_recv.at[slot, a_index, :, columns],
-            y_send_sem.at[b_index, a_index, piece],
-            y_recv_sem.at[slot, a_index, piece],
-            at(a, b_index, core),
-        )
-
-    def y_total(a_index, piece):
-        columns = columns_of(piece)
+            y_send_sem.at[0],
+            y_recv_sem.at[slot, a_index, part],
+            at(a, target, core),
+        )
+
+    def y_total(a_index, part):
+        columns = part_of(part)
         value = part_send[a_index * near + b, :, columns].astype(f32)
-        for b_index in near_order:
-            y_copy(a_index, b_index, b_index, piece).wait_recv()
-            value = value + y_recv[b_index, a_index, :, columns].astype(f32)
+        for step in near_steps:
+            y_copy(a_index, step, step - 1, part).wait_recv()
+            value = value + y_recv[step - 1, a_index, :, columns].astype(f32)
         return value
 
-    def z_copy(a_index, rightward, target, piece):
-        columns = columns_of(piece)
+    def z_copy(a_index, slot, part):
+        columns = part_of(part)
         return remote(
             z_send.at[a_index, :, columns],
-            z_recv.at[rightward, a_index, :, columns],
-            z_send_sem.at[a_index, piece],
-            z_recv_sem.at[rightward, a_index, piece],
-            at(target, b, core),
-        )
-
-    far_targets = [far_first(step) for step in range(far - 1)]
-    for a_index in far_targets + [a]:
-        for piece in range(pieces):
-            for b_index in near_order:
-                y_copy(a_index, b_index, b, piece).start()
-    z_sends = []
-    for a_index in far_targets:
-        rightward = (a_index - a + far) // far
-        following = a + 2 * rightward - 1
-        behind = rightward * a + (1 - rightward) * (far - 1 - a)
-        for piece in range(pieces):
-            columns = columns_of(piece)
-            value = y_total(a_index, piece)
-            copy = z_copy(a_index, rightward, following, piece)
-            z_sends.append(copy)
-
-            @pl.when(behind == 0)
-            def _():
-                z_send[a_index, :, columns] = value.astype(half)
-
-            @pl.when(behind > 0)
-            def _():
-                copy.wait_recv()
-                z_send[a_index, :, columns] = (
-                    value + z_recv[rightward, a_index, :, columns].astype(f32)
-                ).astype(half)
-
-            copy.start()
-    for piece in range(pieces):
-        columns = columns_of(piece)
-        token_sum[:, columns] = y_total(a, piece)
-
-        @pl.when(a > 0)
-        def _():
-            z_copy(a, 1, a, piece).wait_recv()
-            token_sum[:, columns] = token_sum[:, columns] + z_recv[1, a, :, columns].astype(f32)
-
-        @pl.when(a < far - 1)
-        def _():
-            z_copy(a, 0, a, piece).wait_recv()
-            token_sum[:, columns] = token_sum[:, columns] + z_recv[0, a, :, columns].astype(f32)
-
-    tokens = token_sum[...].astype(half)
+            z_recv.at[slot, :, columns],
+            z_send_sem.at[0],
+            z_recv_sem.at[slot, part],
+            at(a_index, b, core),
+        )
+
+    far_targets = [paired(step) for step in range(far - 1, 0, -1)]
+    for part in range(parts):
+        for a_index in far_targets + [a]:
+            for step in near_steps:
+                y_copy(a_index, step, near - step - 1, part).start()
+
+    def merge_far(part):
+        for a_index in far_targets:
+            z_send[a_index, :, part_of(part)] = y_total(a_index, part).astype(half)
+            z_copy(a_index, a, part).start()
+
+    def merge_own(part):
+        columns = part_of(part)
+        value = y_total(a, part)
+        for a_index in far_targets:
+            z_copy(a_index, a_index, part).wait_recv()
+            value = value + z_recv[a_index, :, columns].astype(f32)
+        gathered[place, :, columns] = value.astype(half)
 
     lane_count = router_ref.shape[0]
+
+    def span_of(part):
+        extra = lane_count if part == parts - 1 else 0
+        return pl.ds(part * part_width, part_width + extra)
+
+    def share(slot, send_sem, target, part):
+        block = gathered.at[slot, :, span_of(part)]
+        return remote(block, block, send_sem, g_recv_sem.at[slot, part], target)
+
+    def arrived(slot, part):
+        share(slot, gc_send_sem.at[0], other, part).wait_recv()
+
+    def to_far(a_index, part):
+        return share(place, gz_send_sem.at[0], at(a_index, b, core), part)
+
+    def to_near(a_index, step, part):
+        return share(
+            at(a_index, b, core),
+            gy_send_sem.at[0],
+            at(a, lax.rem(b + step, near), core),
+            part,
+        )
+
+    def to_core(a_index, b_index, part):
+        return share(at(a_index, b_index, core), gc_send_sem.at[0], other, part)
+
+    def pass_on(a_index, part):
+        for step in near_steps:
+            to_near(a_index, step, part).start()
+        to_core(a_index, b, part).start()
+
+    def share_own(part):
+        for step in range(1, far):
+            to_far(paired(step), part).start()
+        pass_on(a, part)
+
+    def forward_far(a_index, part):
+        arrived(at(a_index, b, core), part)
+        pass_on(a_index, part)
+
+    def forward_near(a_index, part):
+        for step in near_steps:
+            b_index = lax.rem(b + step, near)
+            arrived(at(a_index, b_index, core), part)
+            to_core(a_index, b_index, part).start()
+
+    for part in range(parts):
+        merge_far(part)
+    for part in range(parts - 1):
+        merge_own(part)
+        share_own(part)
+    merge_own(parts - 1)
+    tokens = gathered[place, :, :out_width]
+
     logits = by_rows(tokens, router_ref[...])
     lane = lax.broadcasted_iota(jnp.int32, (tokens_here, lane_count), 1)
     line = lax.broadcasted_iota(jnp.int32, (lane_count, tokens_here), 0)
@@ -642,44 +678,14 @@
     route = route_scale * gates / gate_sum
     route_high = route.astype(half)
     route_low = (route - route_high.astype(f32)).astype(half)
-    gathered[place, :, :out_width] = tokens
     gathered[place, :, out_width:] = jnp.where(lane < experts, route_high.astype(f32), route_low.astype(f32)).astype(half)
 
-    def share(slot, send_sem, target):
-        return remote(gathered.at[slot], gathered.at[slot], send_sem, g_recv_sem.at[slot], target)
-
-    def arrived(slot):
-        share(slot, gc_send_sem.at[0], other).wait_recv()
-
-    def to_far(a_index):
-        return share(place, gz_send_sem.at[a_index], at(a_index, b, core))
-
-    def to_near(a_index, b_index):
-        return share(
-            at(a_index, b, core), gy_send_sem.at[a_index, b_index], at(a, b_index, core)
-        )
-
-    def to_core(a_index, b_index):
-        return share(
-            at(a_index, b_index, core), gc_send_sem.at[a_index * near + b_index], other
-        )
-
-    def pass_on(a_index):
-        for b_index in near_order:
-            to_near(a_index, b_index).start()
-        to_core(a_index, b).start()
-
-    def paired(step):
-        value, bit = 0, 1
-        while bit < far:
-            mine, theirs = a // bit % 2, step // bit % 2
-            value = value + bit * (mine + theirs - 2 * mine * theirs)
-            bit *= 2
-        return value
-
-    pass_on(a)
-    for step in range(1, far):
-        to_far(paired(step)).start()
+    share_own(parts - 1)
+    for part in range(parts - 1):
+        forward_far(paired(1), part)
+        forward_near(a, part)
+        for step in range(2, far):
+            forward_far(paired(step), part)
     for copy in weight_copies:
         copy.wait()
 
@@ -688,19 +694,20 @@
         return remote(
             expert_part.at[a_index, side, :, :, columns],
             core_recv.at[a_index, :, :, columns],
-            c_send_sem.at[a_index, piece],
+            c_send_sem.at[0],
             c_recv_sem.at[a_index, piece],
             other,
         )
 
-    def y2_copy(a_index, b_index, slot, piece):
+    def y2_copy(a_index, step, slot, piece):
+        target = lax.rem(b + step, near)
         columns = columns_of(piece)
         return remote(
-            core_sum.at[a_index, b_index, :, columns],
+            core_sum.at[a_index, target, :, columns],
             y2_recv.at[slot, a_index, :, columns],
-            y2_send_sem.at[b_index, a_index, piece],
+            y2_send_sem.at[0],
             y2_recv_sem.at[slot, a_index, piece],
-            at(a, b_index, core),
+            at(a, target, core),
         )
 
     def z2_copy(a_index, slot, piece):
@@ -708,7 +715,7 @@
         return remote(
             z2_send.at[a_index, :, columns],
             z2_recv.at[slot, :, columns],
-            z2_send_sem.at[a_index, piece],
+            z2_send_sem.at[0],
             z2_recv_sem.at[slot, piece],
             at(a_index, b, core),
         )
@@ -717,8 +724,8 @@
     expert = place // 2
 
     def y2_start(a_index, piece):
-        for b_index in near_order:
-            y2_copy(a_index, b_index, b, piece).start()
+        for step in near_steps:
+            y2_copy(a_index, step, near - step - 1, piece).start()
 
     def join_cores(a_index, piece):
         columns = columns_of(piece)
@@ -731,9 +738,9 @@
     def y2_total(a_index, piece):
         columns = columns_of(piece)
         value = core_sum[a_index, b, :, columns].astype(f32)
-        for b_index in near_order:
-            y2_copy(a_index, b_index, b_index, piece).wait_recv()
-            value = value + y2_recv[b_index, a_index, :, columns].astype(f32)
+        for step in near_steps:
+            y2_copy(a_index, step, step - 1, piece).wait_recv()
+            value = value + y2_recv[step - 1, a_index, :, columns].astype(f32)
         return value
 
     def join_near(a_index):
@@ -746,15 +753,30 @@
 
         @pl.when(step < far - 1)
         def _():
-            upcoming = paired(step + 1)
-            arrived(at(upcoming, b, core))
-            pass_on(upcoming)
-
-        for b_index in near_order:
-            arrived(at(a_index, b_index, core))
-            to_core(a_index, b_index).start()
-        for b_index in range(near):
-            arrived(at(a_index, b_index, 1 - core))
+            forward_far(paired(step + 1), parts - 1)
+
+        forward_near(a_index, parts - 1)
+
+        @pl.when(step < far - 1)
+        def _():
+            for part in range(parts - 1):
+                forward_near(paired(step + 1), part)
+
+        @pl.when(step == 1)
+        def _():
+            for piece in range(pieces):
+                join_cores(a, piece)
+
+        @pl.when(step > 1)
+        def _():
+            previous = paired(step - 1)
+            for piece in range(pieces):
+                join_cores(previous, piece)
+                y2_start(previous, piece)
+
+        for part in range(parts):
+            for b_index in range(near):
+                arrived(at(a_index, b_index, 1 - core), part)
         slots = pl.ds(a_index * chunk, chunk)
         rows = gathered[slots, :, :out_width].reshape(chunk * tokens_here, out_width)
         table = gathered[slots, :, out_width:].reshape(chunk * tokens_here, lane_count).astype(f32)
@@ -764,18 +786,6 @@
         gate_part = by_rows(rows, w_gate[...])
         up_part = by_rows(rows, w_up[...])
         hidden_rows[...] = (gate_part / (1.0 + jnp.exp(-gate_part)) * up_part).astype(half)
-
-        @pl.when(step == 1)
-        def _():
-            for piece in range(pieces):
-                join_cores(a, piece)
-
-        @pl.when(step > 1)
-        def _():
-            previous = paired(step - 1)
-            for piece in range(pieces):
-                join_cores(previous, piece)
-                y2_start(previous, piece)
 
         hidden = hidden_rows[...]
         for piece in range(pieces):
@@ -813,22 +823,17 @@
             value = value + z2_recv[paired(step), :, columns].astype(f32)
         out_ref[:, columns] = value.astype(half)
 
-    for copy in z_sends:
-        copy.wait_send()
-    for step in range(1, far):
-        to_far(paired(step)).wait_send()
-        for piece in range(pieces):
-            z2_copy(paired(step), a, piece).wait_send()
-    for a_index in range(far):
-        for piece in range(pieces):
-            core_copy(a_index, 1 - core, piece).wait_send()
-        for b_index in range(near):
-            to_core(a_index, b_index).wait_send()
-        for b_index in near_order:
-            to_near(a_index, b_index).wait_send()
-            for piece in range(pieces):
-                y_copy(a_index, b_index, b, piece).wait_send()
-                y2_copy(a_index, b_index, b, piece).wait_send()
+    def sent(block, sem):
+        remote(block, block, sem, w_recv_sem.at[0], other).wait_send()
+
+    sent(part_send.at[pl.ds(0, far * (near - 1))], y_send_sem.at[0])
+    sent(z_send.at[pl.ds(0, far - 1)], z_send_sem.at[0])
+    sent(gathered.at[pl.ds(0, far - 1)], gz_send_sem.at[0])
+    sent(gathered.at[pl.ds(0, far * (near - 1))], gy_send_sem.at[0])
+    sent(gathered.at[pl.ds(0, chips)], gc_send_sem.at[0])
+    sent(core_sum, c_send_sem.at[0])
+    sent(y2_recv, y2_send_sem.at[0])
+    sent(z2_send.at[pl.ds(0, far - 1)], z2_send_sem.at[0])
 
 
 def layer_kernel(far, near, peers, head_dim, *refs):
@@ -937,16 +942,15 @@
             pltpu.VMEM((chips, rows, 2 * depth), half),
             pltpu.VMEM((chips, rows, 2 * depth), half),
             pltpu.VMEM((chips, *block), half),
-            pltpu.VMEM((near, far, *block), half),
+            pltpu.VMEM((near - 1, far, *block), half),
             pltpu.VMEM((far, *block), half),
-            pltpu.VMEM((2, far, *block), half),
-            pltpu.VMEM(block, jnp.float32),
+            pltpu.VMEM((far, *block), half),
             pltpu.VMEM((devices, rows, out_width + lanes), half),
             pltpu.VMEM((2 * near * rows, hidden), half),
             pltpu.VMEM((far, 2, near, *block), half),
             pltpu.VMEM((far, near, *block), half),
             pltpu.VMEM((far, near, *block), half),
-            pltpu.VMEM((near, far, *block), half),
+            pltpu.VMEM((near - 1, far, *block), half),
             pltpu.VMEM((far, *block), half),
             pltpu.VMEM((far, *block), half),
             dma((5,)),
@@ -954,19 +958,19 @@
             dma((1,)),
             dma((chips,)),
             dma((chips,)),
-            dma((near, far, pieces)),
-            dma((near, far, pieces)),
+            dma((1,)),
+            dma((near - 1, far, column_parts)),
+            dma((1,)),
+            dma((far, column_parts)),
+            dma((devices, column_parts)),
+            dma((1,)),
+            dma((1,)),
+            dma((1,)),
+            dma((1,)),
             dma((far, pieces)),
-            dma((2, far, pieces)),
-            dma((devices,)),
-            dma((far,)),
-            dma((far, near)),
-            dma((chips,)),
-            dma((far, pieces)),
-            dma((far, pieces)),
-            dma((near, far, pieces)),
-            dma((near, far, pieces)),
-            dma((far, pieces)),
+            dma((1,)),
+            dma((near - 1, far, pieces)),
+            dma((1,)),
             dma((far, pieces)),
         ],
         compiler_params=pltpu.CompilerParams(

time: 100 us -> 95.9 us (0.959)
  Pallas kernels: 98 us -> 93.4 us
    pallas_call x1, Pallas kernels: 98 us -> 93.4 us  [fast_local(): pl.pallas_call(functools.partial(layer_kernel, far, near, peers, head_dim...]
where the time goes in v2:
time: 95.9 us; the launch traced here: 94.9 us
  Pallas kernels  93.4 us (97%)
  local copies, waits for them, and re-layouts  1.57 us (2%)
    pallas_call x1, Pallas kernels, fast_local(): pl.pallas_call(functools.partial(layer_kernel, far, near, peers, head_dim...  93.4 us

profile of v2, /device:TPU:0, one launch (start us, length us, event | category | flops | bytes accessed | tf_op | source)
XLA Modules:
  0.0 94.9 jit_solution(13634567663904501365)
XLA Ops:
  0.0 93.4 %layer.1 = bf16[32,2048]{1,0:T(8,128)(2,1)} custom-call(s32[2,2]{1,0:T(2,128)} %refs_0_.1, bf16[128,3456]{1,0:T(8,128)(2,1)} %refs_1_.1, bf16[1152,1152]{1,0:T(8,128)(2,1)} %refs_2_.1, f32[36,128]{1,0:T(8,128)} %bitcast.9, f32[36,128]{1,0:T(8,128)} %bitcast.10, s32[6,32]{1,0:T(8,128)} %bitcast.11, bf16[8,2048]{1,0:T(8,128)(2,1)} %bitcast.8, ...), custom_call_target="tpu_custom_call" | custom-call | tf_op jit(solution)/shard_map/layer/pallas_call | solution.py:903
  93.4 1.6 %copy.13 = bf16[32,2048]{1,0:T(8,128)(2,1)} copy(bf16[32,2048]{1,0:T(8,128)(2,1)} %layer.1) | data formatting | bytes 262144

commit v3 on v2

--- a/solution.py
+++ b/solution.py
@@ -248,10 +248,15 @@
     bias_ref,
     out_ref,
     qkv_ref,
-    send,
-    recv,
+    pair_send,
+    pair_recv,
+    value_send,
+    value_recv,
+    queries,
     keys,
     values,
+    weights_kept,
+    sums_kept,
     mixed_send,
     mixed_recv,
     attention,
@@ -277,33 +282,65 @@
     weight_copy = pltpu.make_async_copy(w_out_hbm, w_out_ref, local_sem.at[0])
     weight_copy.start()
     qkv_copy.wait()
-    for peer in range(peers):
-        for part in range(3):
-            start = part * width + peer * span
-            send[peer, :, part * span : (part + 1) * span] = qkv_ref[:, start : start + span]
+    tail = span - 128
+    for part, (packed, first, last) in enumerate(
+        [
+            (pair_send, 0, 2 * rows),
+            (pair_send, rows, 2 * rows + tail),
+            (value_send, 0, rows),
+        ]
+    ):
+        ends = [part * width + (peer + 1) * span for peer in range(peers)]
+        tails = jnp.concatenate([qkv_ref[:, end - tail : end] for end in ends], axis=1)
+        turned = tails.astype(jnp.float32).T
+        for peer, end in enumerate(ends):
+            packed[peer, first : first + rows, :] = qkv_ref[:, end - span : end - tail]
+            packed[peer, last : last + tail, :] = turned[
+                peer * tail : (peer + 1) * tail
+            ].astype(jnp.bfloat16)
     pl.semaphore_wait(barrier, devices - 1)
-    own = pltpu.make_async_copy(send.at[me], recv.at[me], local_sem.at[1])
-    own.start()
-    sends = []
-    for step in range(1, peers):
-        peer = lax.rem(me + step, peers)
-        copy = remote(
-            send.at[peer], recv.at[me], send_sem.at[peer], recv_sem.at[me], base + peer
-        )
-        copy.start()
-        sends.append(copy)
+    own_pair = pltpu.make_async_copy(pair_send.at[me], pair_recv.at[me], local_sem.at[1])
+    own_value = pltpu.make_async_copy(value_send.at[me], value_recv.at[me], local_sem.at[4])
+    own_pair.start()
+    own_value.start()
+    for kind, (source, target) in enumerate(
+        [(pair_send, pair_recv), (value_send, value_recv)]
+    ):
+        for step in range(1, peers):
+            peer = lax.rem(me + step, peers)
+            remote(
+                source.at[peer], target.at[me], send_sem.at[kind], recv_sem.at[kind], base + peer
+            ).start()
     start_rest()
-    own.wait()
-    for step in range(1, peers):
-        peer = lax.rem(me + step, peers)
-        remote(
-            send.at[peer], recv.at[peer], send_sem.at[peer], recv_sem.at[peer], base + peer
-        ).wait_recv()
-    for head in range(heads):
-        low = span + head * head_dim
-        keys[head] = recv[:, :, low : low + head_dim].reshape(peers * rows, head_dim)
-        low = 2 * span + head * head_dim
-        values[head] = recv[:, :, low : low + head_dim].reshape(peers * rows, head_dim)
+
+    def whole(block, kind):
+        block = block.at[pl.ds(0, peers - 1)]
+        return remote(
+            block, block, send_sem.at[kind], recv_sem.at[kind], base + lax.rem(me + 1, peers)
+        )
+
+    own_pair.wait()
+    whole(pair_recv, 0).wait_recv()
+
+    def unpack(packed, first, last, target):
+        turned = (
+            packed[:, last : last + tail, :].astype(jnp.float32).reshape(peers * tail, rows).T
+        )
+        for peer in range(peers):
+            joined = jnp.concatenate(
+                [
+                    packed[peer, first : first + rows, :],
+                    turned[:, peer * tail : (peer + 1) * tail].astype(jnp.bfloat16),
+                ],
+                axis=1,
+            )
+            for head in range(heads):
+                target[head, peer * rows : (peer + 1) * rows, :] = joined[
+                    :, head * head_dim : (head + 1) * head_dim
+                ]
+
+    unpack(pair_recv, 0, 2 * rows, queries)
+    unpack(pair_recv, rows, 2 * rows + tail, keys)
     factor = head_dim ** (-0.5) * 1.4426950408889634
     clip = place // peers
     count = grid_ref[clip, 0] * grid_ref[clip, 1]
@@ -312,25 +349,33 @@
     group = 2 if peers % 2 == 0 else 1
     blocks = peers // group
 
-    def one_block(step, carry):
-        block = lax.rem(me // group + 1 + step, blocks)
-        outcomes = []
+    def score_block(block, carry):
+        lines = pl.ds(pl.multiple_of(block * group * rows, group * rows), group * rows)
         for head in range(heads):
-            low = head * head_dim
-            query = recv[pl.ds(block * group, group), :, low : low + head_dim].reshape(
-                group * rows, head_dim
-            )
             scores = lax.dot_general(
-                query, keys[head], (((1,), (1,)), ((), ())), preferred_element_type=jnp.float32
+                queries[head, lines, :], keys[head], (((1,), (1,)), ((), ())), preferred_element_type=jnp.float32
             )
             scores = scores + hide
             highest = jnp.max(scores, axis=1, keepdims=True)
             weights = jnp.exp2((scores - highest) * factor)
-            running = jnp.sum(weights, axis=1, keepdims=True)
+            sums_kept[head, lines, :] = jnp.sum(weights, axis=1, keepdims=True)
+            weights_kept[head, lines, :] = weights.astype(jnp.bfloat16)
+        return carry
+
+    lax.fori_loop(0, blocks, score_block, 0)
+    own_value.wait()
+    whole(value_recv, 1).wait_recv()
+    unpack(value_recv, 0, rows, values)
+
+    def one_block(step, carry):
+        block = lax.rem(me // group + 1 + step, blocks)
+        lines = pl.ds(pl.multiple_of(block * group * rows, group * rows), group * rows)
+        outcomes = []
+        for head in range(heads):
             mixture = jnp.dot(
-                weights.astype(jnp.bfloat16), values[head], preferred_element_type=jnp.float32
+                weights_kept[head, lines, :], values[head], preferred_element_type=jnp.float32
             )
-            outcomes.append((mixture / running).astype(jnp.bfloat16))
+            outcomes.append((mixture / sums_kept[head, lines, :]).astype(jnp.bfloat16))
         joined = jnp.concatenate([piece.astype(jnp.float32) for piece in outcomes], axis=1)
         for part in range(group):
             peer = block * group + part
@@ -346,8 +391,8 @@
                 remote(
                     mixed_send.at[peer],
                     mixed_recv.at[me],
-                    back_send_sem.at[peer],
-                    back_recv_sem.at[me],
+                    back_send_sem.at[0],
+                    back_recv_sem.at[0],
                     base + peer,
                 ).start()
 
@@ -361,19 +406,18 @@
 
     lax.fori_loop(0, blocks, one_block, 0)
     pltpu.make_async_copy(mixed_send.at[me], mixed_recv.at[me], local_sem.at[2]).wait()
-    for step in range(1, peers):
-        peer = lax.rem(me + step, peers)
-        copy = remote(
-            mixed_send.at[peer],
-            mixed_recv.at[peer],
-            back_send_sem.at[peer],
-            back_recv_sem.at[peer],
-            base + peer,
-        )
-        copy.wait_recv()
-        copy.wait_send()
-    for copy in sends:
-        copy.wait_send()
+    returned = mixed_recv.at[pl.ds(0, peers - 1)]
+    back = remote(
+        returned,
+        returned,
+        back_send_sem.at[0],
+        back_recv_sem.at[0],
+        base + lax.rem(me + 1, peers),
+    )
+    back.wait_recv()
+    back.wait_send()
+    whole(pair_send, 0).wait_send()
+    whole(value_send, 1).wait_send()
     for peer in range(peers):
         start = peer * span
         attention[:, start : start + 128] = mixed_recv[peer, :rows, :]
@@ -431,7 +475,7 @@
     z_send,
     z_recv,
     gathered,
-    hidden_rows,
+    gate_rows,
     expert_part,
     core_recv,
     core_sum,
@@ -507,7 +551,7 @@
     own_norm.start()
     for q in other_chips:
         remote(
-            norm_send.at[q], norm_recv.at[chip], n_send_sem.at[q], n_recv_sem.at[chip], q * 2 + core
+            norm_send.at[q], norm_recv.at[chip], n_send_sem.at[0], n_recv_sem.at[0], q * 2 + core
         ).start()
     merge_copy.wait()
     merge_swap.wait_send()
@@ -519,12 +563,10 @@
         other,
     ).wait_recv()
     own_norm.wait()
-    for q in other_chips:
-        copy = remote(
-            norm_send.at[q], norm_recv.at[q], n_send_sem.at[q], n_recv_sem.at[q], q * 2 + core
-        )
-        copy.wait_recv()
-        copy.wait_send()
+    arrivals = norm_recv.at[pl.ds(0, chips - 1)]
+    normed_copies = remote(arrivals, arrivals, n_send_sem.at[0], n_recv_sem.at[0], other)
+    normed_copies.wait_recv()
+    normed_copies.wait_send()
     column_block = min(512, out_width)
     flat = norm_recv[...].reshape(chips * tokens_here, 2 * depth)
 
@@ -638,9 +680,17 @@
             to_near(a_index, step, part).start()
         to_core(a_index, b, part).start()
 
+    def turn(step):
+        value, bit = 0, 1
+        while bit < far:
+            wide_bit, next_bit = far // (2 * bit), far // bit
+            value = value + bit * ((step // wide_bit + step // next_bit) % 2)
+            bit *= 2
+        return paired(value)
+
     def share_own(part):
         for step in range(1, far):
-            to_far(paired(step), part).start()
+            to_far(turn(step), part).start()
         pass_on(a, part)
 
     def forward_far(a_index, part):
@@ -682,10 +732,10 @@
 
     share_own(parts - 1)
     for part in range(parts - 1):
-        forward_far(paired(1), part)
+        forward_far(turn(1), part)
         forward_near(a, part)
         for step in range(2, far):
-            forward_far(paired(step), part)
+            forward_far(turn(step), part)
     for copy in weight_copies:
         copy.wait()
 
@@ -749,18 +799,18 @@
             z2_copy(a_index, a, piece).start()
 
     def chunks(step, carry):
-        a_index = paired(step)
+        a_index = turn(step)
 
         @pl.when(step < far - 1)
         def _():
-            forward_far(paired(step + 1), parts - 1)
+            forward_far(turn(step + 1), parts - 1)
 
         forward_near(a_index, parts - 1)
 
         @pl.when(step < far - 1)
         def _():
             for part in range(parts - 1):
-                forward_near(paired(step + 1), part)
+                forward_near(turn(step + 1), part)
 
         @pl.when(step == 1)
         def _():
@@ -769,7 +819,7 @@
 
         @pl.when(step > 1)
         def _():
-            previous = paired(step - 1)
+            previous = turn(step - 1)
             for piece in range(pieces):
                 join_cores(previous, piece)
                 y2_start(previous, piece)
@@ -783,11 +833,11 @@
         table_lane = lax.broadcasted_iota(jnp.int32, table.shape, 1)
         mine = jnp.logical_or(table_lane == expert, table_lane == expert + experts)
         scale = jnp.sum(jnp.where(mine, table, 0.0), axis=1, keepdims=True)
-        gate_part = by_rows(rows, w_gate[...])
+        gate_rows[...] = by_rows(rows, w_gate[...])
+        gate_part = gate_rows[...]
         up_part = by_rows(rows, w_up[...])
-        hidden_rows[...] = (gate_part / (1.0 + jnp.exp(-gate_part)) * up_part).astype(half)
-
-        hidden = hidden_rows[...]
+        hidden = (gate_part / (1.0 + jnp.exp(-gate_part)) * up_part).astype(half)
+
         for piece in range(pieces):
             columns = columns_of(piece)
             product = jnp.dot(hidden, w_down[:, columns], preferred_element_type=f32).astype(half)
@@ -802,25 +852,25 @@
 
         @pl.when(step > 2)
         def _():
-            join_near(paired(step - 2))
+            join_near(turn(step - 2))
 
         return carry
 
     lax.fori_loop(0, far, chunks, 0)
-    final = paired(far - 1)
+    final = turn(far - 1)
     for piece in range(pieces):
         join_cores(final, piece)
         y2_start(final, piece)
     for piece in range(pieces):
         y2_start(a, piece)
     for step in range(max(1, far - 2), far):
-        join_near(paired(step))
+        join_near(turn(step))
     for piece in range(pieces):
         columns = columns_of(piece)
         value = y2_total(a, piece)
         for step in range(1, far):
-            z2_copy(paired(step), paired(step), piece).wait_recv()
-            value = value + z2_recv[paired(step), :, columns].astype(f32)
+            z2_copy(turn(step), turn(step), piece).wait_recv()
+            value = value + z2_recv[turn(step), :, columns].astype(f32)
         out_ref[:, columns] = value.astype(half)
 
     def sent(block, sem):
@@ -840,7 +890,7 @@
     operands, out_ref, normed = refs[:11], refs[11], refs[12]
     grid_ref, qkv_hbm, w_out_hbm, gain_ref, bias_ref = operands[:5]
     scratch = refs[13:]
-    vision_scratch, language_scratch = scratch[:15], scratch[15:]
+    vision_scratch, language_scratch = scratch[:20], scratch[20:]
     place = lax.axis_index("wide")
     devices = lax.axis_size("wide")
     barrier = greet([lax.rem(place + step, devices) for step in range(1, devices)])
@@ -920,20 +970,25 @@
         scratch_shapes=[
             pltpu.VMEM((rows, 4 * width), half),
             pltpu.VMEM((patch_rows, 3 * width), half),
-            pltpu.VMEM((peers, patch_rows, 3 * span), half),
-            pltpu.VMEM((peers, patch_rows, 3 * span), half),
+            pltpu.VMEM((peers, 2 * (patch_rows + span - 128), 128), half),
+            pltpu.VMEM((peers, 2 * (patch_rows + span - 128), 128), half),
+            pltpu.VMEM((peers, patch_rows + span - 128, 128), half),
+            pltpu.VMEM((peers, patch_rows + span - 128, 128), half),
             pltpu.VMEM((heads, peers * patch_rows, head_dim), half),
             pltpu.VMEM((heads, peers * patch_rows, head_dim), half),
+            pltpu.VMEM((heads, peers * patch_rows, head_dim), half),
+            pltpu.VMEM((heads, peers * patch_rows, peers * patch_rows), half),
+            pltpu.VMEM((heads, peers * patch_rows, 1), jnp.float32),
             pltpu.VMEM((peers, patch_rows + span - 128, 128), half),
             pltpu.VMEM((peers, patch_rows + span - 128, 128), half),
             pltpu.VMEM((patch_rows, width), half),
             pltpu.VMEM((width // 128, patch_rows, 128), jnp.float32),
             pltpu.VMEM((width, width), half),
-            dma((peers,)),
-            dma((peers,)),
-            dma((peers,)),
-            dma((peers,)),
-            dma((4,)),
+            dma((2,)),
+            dma((2,)),
+            dma((1,)),
+            dma((1,)),
+            dma((5,)),
             pltpu.VMEM((lanes, out_width), half),
             pltpu.VMEM((2 * depth, out_width), half),
             pltpu.VMEM((hidden, out_width), half),
@@ -946,7 +1001,7 @@
             pltpu.VMEM((far, *block), half),
             pltpu.VMEM((far, *block), half),
             pltpu.VMEM((devices, rows, out_width + lanes), half),
-            pltpu.VMEM((2 * near * rows, hidden), half),
+            pltpu.VMEM((2 * near * rows, hidden), jnp.float32),
             pltpu.VMEM((far, 2, near, *block), half),
             pltpu.VMEM((far, near, *block), half),
             pltpu.VMEM((far, near, *block), half),
@@ -956,8 +1011,8 @@
             dma((5,)),
             dma((1,)),
             dma((1,)),
-            dma((chips,)),
-            dma((chips,)),
+            dma((1,)),
+            dma((1,)),
             dma((1,)),
             dma((near - 1, far, column_parts)),
             dma((1,)),

time: 95.9 us -> 93.6 us (0.976)
  Pallas kernels: 93.4 us -> 91.9 us
    pallas_call x1, Pallas kernels: 93.4 us -> 91.9 us  [fast_local(): pl.pallas_call(functools.partial(layer_kernel, far, near, peers, head_dim...]
where the time goes in v3:
time: 93.6 us; the launch traced here: 93.5 us
  Pallas kernels  91.9 us (98%)
  local copies, waits for them, and re-layouts  1.57 us (2%)
    pallas_call x1, Pallas kernels, fast_local(): pl.pallas_call(functools.partial(layer_kernel, far, near, peers, head_dim...  91.9 us

profile of v3, /device:TPU:0, one launch (start us, length us, event | category | flops | bytes accessed | tf_op | source)
XLA Modules:
  0.0 93.5 jit_solution(744294796076397473)
XLA Ops:
  0.0 91.9 %layer.1 = bf16[32,2048]{1,0:T(8,128)(2,1)} custom-call(s32[2,2]{1,0:T(2,128)} %refs_0_.1, bf16[128,3456]{1,0:T(8,128)(2,1)} %refs_1_.1, bf16[1152,1152]{1,0:T(8,128)(2,1)} %refs_2_.1, f32[36,128]{1,0:T(8,128)} %bitcast.9, f32[36,128]{1,0:T(8,128)} %bitcast.10, s32[6,32]{1,0:T(8,128)} %bitcast.11, bf16[8,2048]{1,0:T(8,128)(2,1)} %bitcast.8, ...), custom_call_target="tpu_custom_call" | custom-call | tf_op jit(solution)/shard_map/layer/pallas_call | solution.py:953
  91.9 1.6 %copy.13 = bf16[32,2048]{1,0:T(8,128)(2,1)} copy(bf16[32,2048]{1,0:T(8,128)(2,1)} %layer.1) | data formatting | bytes 262144

commit v4 on v3

--- a/solution.py
+++ b/solution.py
@@ -268,6 +268,7 @@
     back_recv_sem,
     local_sem,
     start_rest,
+    fetches,
 ):
     place = lax.axis_index("wide")
     base = place // peers * peers
@@ -281,6 +282,8 @@
     qkv_copy.start()
     weight_copy = pltpu.make_async_copy(w_out_hbm, w_out_ref, local_sem.at[0])
     weight_copy.start()
+    for fetch in fetches:
+        fetch.start()
     qkv_copy.wait()
     tail = span - 128
     for part, (packed, first, last) in enumerate(
@@ -311,6 +314,8 @@
             remote(
                 source.at[peer], target.at[me], send_sem.at[kind], recv_sem.at[kind], base + peer
             ).start()
+    for fetch in fetches:
+        fetch.wait()
     start_rest()
 
     def whole(block, kind):
@@ -368,7 +373,10 @@
     unpack(value_recv, 0, rows, values)
 
     def one_block(step, carry):
-        block = lax.rem(me // group + 1 + step, blocks)
+        block, bit = 0, 1
+        while bit < blocks:
+            block = block + bit * ((me // group // bit + (blocks - 1 - step) // bit) % 2)
+            bit *= 2
         lines = pl.ds(pl.multiple_of(block * group * rows, group * rows), group * rows)
         outcomes = []
         for head in range(heads):
@@ -888,12 +896,25 @@
 
 def layer_kernel(far, near, peers, head_dim, *refs):
     operands, out_ref, normed = refs[:11], refs[11], refs[12]
-    grid_ref, qkv_hbm, w_out_hbm, gain_ref, bias_ref = operands[:5]
-    scratch = refs[13:]
+    grid_ref, gain_ref, bias_ref, ids_ref, named_ref, small_sem = refs[13:19]
+    grid_hbm, qkv_hbm, w_out_hbm, gain_hbm, bias_hbm, ids_hbm, named_hbm = operands[:7]
+    scratch = refs[19:]
     vision_scratch, language_scratch = scratch[:20], scratch[20:]
     place = lax.axis_index("wide")
     devices = lax.axis_size("wide")
     barrier = greet([lax.rem(place + step, devices) for step in range(1, devices)])
+    fetches = [
+        pltpu.make_async_copy(source, target, small_sem.at[index])
+        for index, (source, target) in enumerate(
+            [
+                (named_hbm, named_ref),
+                (grid_hbm, grid_ref),
+                (gain_hbm, gain_ref),
+                (bias_hbm, bias_ref),
+                (ids_hbm, ids_ref),
+            ]
+        )
+    ]
 
     def run_vision(start_rest):
         vision_part(
@@ -908,9 +929,20 @@
             normed,
             *vision_scratch,
             start_rest,
-        )
-
-    language_part(far, near, run_vision, normed, *operands[5:], out_ref, *language_scratch)
+            fetches,
+        )
+
+    language_part(
+        far,
+        near,
+        run_vision,
+        normed,
+        ids_ref,
+        named_ref,
+        *operands[7:],
+        out_ref,
+        *language_scratch,
+    )
 
 
 def fast_local(
@@ -945,7 +977,7 @@
     lanes = -(-2 * experts // 128) * 128
     hidden = w_gate.shape[2]
     whole = pl.BlockSpec(memory_space=pltpu.VMEM)
-    away = pl.BlockSpec(memory_space=pl.ANY)
+    away = pl.BlockSpec(memory_space=pltpu.MemorySpace.HBM)
     half = jnp.bfloat16
     block = (rows, out_width)
     dma = pltpu.SemaphoreType.DMA
@@ -953,22 +985,16 @@
     return pl.pallas_call(
         functools.partial(layer_kernel, far, near, peers, head_dim),
         out_shape=jax.ShapeDtypeStruct(block, half),
-        in_specs=[
-            pl.BlockSpec(memory_space=pltpu.SMEM),
-            away,
-            away,
-            whole,
-            whole,
-            whole,
-            whole,
-            away,
-            away,
-            away,
-            away,
-        ],
+        in_specs=[away] * 11,
         out_specs=whole,
         scratch_shapes=[
             pltpu.VMEM((rows, 4 * width), half),
+            pltpu.SMEM(grid.shape, jnp.int32),
+            pltpu.VMEM((4 * width // 128, 128), jnp.float32),
+            pltpu.VMEM((4 * width // 128, 128), jnp.float32),
+            pltpu.VMEM(expert_ids.shape[::-1], jnp.int32),
+            pltpu.VMEM((experts, out_width), half),
+            dma((5,)),
             pltpu.VMEM((patch_rows, 3 * width), half),
             pltpu.VMEM((peers, 2 * (patch_rows + span - 128), 128), half),
             pltpu.VMEM((peers, 2 * (patch_rows + span - 128), 128), half),
@@ -1029,21 +1055,26 @@
             dma((far, pieces)),
         ],
         compiler_params=pltpu.CompilerParams(
-            collective_id=0, has_side_effects=True, vmem_limit_bytes=62 * 2**20
+            collective_id=0, has_side_effects=True, vmem_limit_bytes=50 * 2**20
         ),
         name="layer",
     )(
-        grid,
-        qkv,
-        w_out,
-        ln_gain.reshape(-1, 128),
-        ln_bias.reshape(-1, 128),
-        expert_ids.T,
-        w_router.T,
-        w_merge,
-        w_gate.swapaxes(1, 2),
-        w_up.swapaxes(1, 2),
-        w_down,
+        *[
+            pltpu.with_memory_space_constraint(operand, pltpu.MemorySpace.HBM)
+            for operand in (
+                grid,
+                qkv,
+                w_out,
+                ln_gain.reshape(-1, 128),
+                ln_bias.reshape(-1, 128),
+                expert_ids.T,
+                w_router.T,
+                w_merge,
+                w_gate.swapaxes(1, 2),
+                w_up.swapaxes(1, 2),
+                w_down,
+            )
+        ]
     )
 
 

time: 93.6 us -> 91.3 us (0.975)
  Pallas kernels: 91.9 us -> 90.5 us
    pallas_call x1, Pallas kernels: 91.9 us -> 90.5 us  [fast_local(): pl.pallas_call(functools.partial(layer_kernel, far, near, peers, head_dim...]
where the time goes in v4:
time: 91.3 us; the launch traced here: 91.1 us
  Pallas kernels  90.5 us (99%)
    pallas_call x1, Pallas kernels, fast_local(): pl.pallas_call(functools.partial(layer_kernel, far, near, peers, head_dim...  90.5 us

profile of v4, /device:TPU:0, one launch (start us, length us, event | category | flops | bytes accessed | tf_op | source)
XLA Modules:
  0.0 91.1 jit_solution(17204306005615714789)
XLA Ops:
  0.0 90.5 %layer.1 = bf16[32,2048]{1,0:T(8,128)(2,1)S(1)} custom-call(s32[2,2]{1,0:T(2,128)} %refs_0_.1, bf16[128,3456]{1,0:T(8,128)(2,1)} %refs_1_.1, bf16[1152,1152]{1,0:T(8,128)(2,1)} %refs_2_.1, f32[36,128]{1,0:T(8,128)} %bitcast.9, f32[36,128]{1,0:T(8,128)} %bitcast.10, s32[6,32]{1,0:T(8,128)} %bitcast.11, bf16[8,2048]{1,0:T(8,128)(2,1)} %bitcast.8, ...), custom_call_target="tpu_custom_call" | custom-call | tf_op jit(solution)/shard_map/layer/pallas_call | solution.py:985
  90.5 0.7 copy.13

commit v5 on v4

--- a/solution.py
+++ b/solution.py
@@ -482,8 +482,8 @@
     y_recv,
     z_send,
     z_recv,
+    chosen_kept,
     gathered,
-    gate_rows,
     expert_part,
     core_recv,
     core_sum,
@@ -553,8 +553,19 @@
         ).astype(half)
 
     run_vision(start_rest)
+    tiles, rest = divmod(2 * depth, 128)
+    folds = 128 // rest
+    folded = tokens_here // folds
     for q in range(chips):
-        norm_send[q] = normed_ref[:, 2 * depth * q : 2 * depth * (q + 1)]
+        low = 2 * depth * q
+        for tile in range(tiles):
+            norm_send[q, tile * tokens_here : (tile + 1) * tokens_here, :] = normed_ref[
+                :, low + tile * 128 : low + (tile + 1) * 128
+            ]
+        end = normed_ref[:, low + tiles * 128 : low + 2 * depth]
+        norm_send[q, tiles * tokens_here :, :] = jnp.concatenate(
+            [end[fold * folded : (fold + 1) * folded] for fold in range(folds)], axis=1
+        )
     own_norm = pltpu.make_async_copy(norm_send.at[chip], norm_recv.at[chip], local_sem.at[4])
     own_norm.start()
     for q in other_chips:
@@ -576,7 +587,20 @@
     normed_copies.wait_recv()
     normed_copies.wait_send()
     column_block = min(512, out_width)
-    flat = norm_recv[...].reshape(chips * tokens_here, 2 * depth)
+    end = norm_recv[:, tiles * tokens_here :, :]
+    end = jnp.concatenate(
+        [end[:, :, fold * rest : (fold + 1) * rest] for fold in range(folds)], axis=1
+    )
+    flat = jnp.concatenate(
+        [
+            norm_recv[:, tile * tokens_here : (tile + 1) * tokens_here, :].reshape(
+                chips * tokens_here, 128
+            )
+            for tile in range(tiles)
+        ]
+        + [end.reshape(chips * tokens_here, rest)],
+        axis=1,
+    )
 
     def merge_columns(index, carry):
         columns = pl.ds(pl.multiple_of(index * column_block, column_block), column_block)
@@ -711,15 +735,6 @@
             arrived(at(a_index, b_index, core), part)
             to_core(a_index, b_index, part).start()
 
-    for part in range(parts):
-        merge_far(part)
-    for part in range(parts - 1):
-        merge_own(part)
-        share_own(part)
-    merge_own(parts - 1)
-    tokens = gathered[place, :, :out_width]
-
-    logits = by_rows(tokens, router_ref[...])
     lane = lax.broadcasted_iota(jnp.int32, (tokens_here, lane_count), 1)
     line = lax.broadcasted_iota(jnp.int32, (lane_count, tokens_here), 0)
     line = jnp.where(line < experts, line, line - experts)
@@ -731,7 +746,17 @@
         == lax.broadcasted_iota(jnp.int32, (tokens_here, tokens_here), 1)
     )
     chosen = by_rows(jnp.where(same, 1.0, 0.0).astype(half), marks.astype(half))
-    gates = chosen / (1.0 + jnp.exp(-logits))
+    chosen_kept[...] = chosen
+    for part in range(parts):
+        merge_far(part)
+    for part in range(parts - 1):
+        merge_own(part)
+        share_own(part)
+    merge_own(parts - 1)
+    tokens = gathered[place, :, :out_width]
+
+    logits = by_rows(tokens, router_ref[...])
+    gates = chosen_kept[...] / (1.0 + jnp.exp(-logits))
     gate_sum = jnp.sum(jnp.where(lane < experts, gates, 0.0), axis=1, keepdims=True)
     route = route_scale * gates / gate_sum
     route_high = route.astype(half)
@@ -841,8 +866,7 @@
         table_lane = lax.broadcasted_iota(jnp.int32, table.shape, 1)
         mine = jnp.logical_or(table_lane == expert, table_lane == expert + experts)
         scale = jnp.sum(jnp.where(mine, table, 0.0), axis=1, keepdims=True)
-        gate_rows[...] = by_rows(rows, w_gate[...])
-        gate_part = gate_rows[...]
+        gate_part = by_rows(rows, w_gate[...])
         up_part = by_rows(rows, w_up[...])
         hidden = (gate_part / (1.0 + jnp.exp(-gate_part)) * up_part).astype(half)
 
@@ -1020,14 +1044,14 @@
             pltpu.VMEM((hidden, out_width), half),
             pltpu.VMEM((hidden, out_width), half),
             pltpu.VMEM((hidden, out_width), half),
-            pltpu.VMEM((chips, rows, 2 * depth), half),
-            pltpu.VMEM((chips, rows, 2 * depth), half),
+            pltpu.VMEM((chips, rows * 2 * depth // 128, 128), half),
+            pltpu.VMEM((chips, rows * 2 * depth // 128, 128), half),
             pltpu.VMEM((chips, *block), half),
             pltpu.VMEM((near - 1, far, *block), half),
             pltpu.VMEM((far, *block), half),
             pltpu.VMEM((far, *block), half),
+            pltpu.VMEM((rows, lanes), jnp.float32),
             pltpu.VMEM((devices, rows, out_width + lanes), half),
-            pltpu.VMEM((2 * near * rows, hidden), jnp.float32),
             pltpu.VMEM((far, 2, near, *block), half),
             pltpu.VMEM((far, near, *block), half),
             pltpu.VMEM((far, near, *block), half),
@@ -1089,6 +1113,8 @@
         return local(*operands)
     span = HEADS // (devices // CLIPS) * (operands[2].shape[0] // HEADS)
     packs = qkv.shape[0] == 128 and 128 < span < 256 and span % 16 == 0
+    rest = 2 * operands[5].shape[0] % 128
+    packs = packs and rest > 0 and 128 % rest == 0 and token_count * rest % 2048 == 0
     return fast_local(*operands) if packs else local(*operands)
 
 

time: 91.3 us -> 90.6 us (level)
  no operation moved by 1% of the time
where the time goes in v5:
time: 90.6 us; the launch traced here: 90.5 us
  Pallas kernels  89.8 us (99%)
    pallas_call x1, Pallas kernels, fast_local(): pl.pallas_call(functools.partial(layer_kernel, far, near, peers, head_dim...  89.8 us

profile of v5, /device:TPU:0, one launch (start us, length us, event | category | flops | bytes accessed | tf_op | source)
XLA Modules:
  0.0 90.5 jit_solution(10871674751732070755)
XLA Ops:
  0.0 89.8 %layer.1 = bf16[32,2048]{1,0:T(8,128)(2,1)S(1)} custom-call(s32[2,2]{1,0:T(2,128)} %refs_0_.1, bf16[128,3456]{1,0:T(8,128)(2,1)} %refs_1_.1, bf16[1152,1152]{1,0:T(8,128)(2,1)} %refs_2_.1, f32[36,128]{1,0:T(8,128)} %bitcast.9, f32[36,128]{1,0:T(8,128)} %bitcast.10, s32[6,32]{1,0:T(8,128)} %bitcast.11, bf16[8,2048]{1,0:T(8,128)(2,1)} %bitcast.8, ...), custom_call_target="tpu_custom_call" | custom-call | tf_op jit(solution)/shard_map/layer/pallas_call | solution.py:1009
  89.8 0.7 copy.13

commit v6 on v5

--- a/solution.py
+++ b/solution.py
@@ -586,7 +586,7 @@
     normed_copies = remote(arrivals, arrivals, n_send_sem.at[0], n_recv_sem.at[0], other)
     normed_copies.wait_recv()
     normed_copies.wait_send()
-    column_block = min(512, out_width)
+    column_block = min(1024, out_width)
     end = norm_recv[:, tiles * tokens_here :, :]
     end = jnp.concatenate(
         [end[:, :, fold * rest : (fold + 1) * rest] for fold in range(folds)], axis=1
@@ -1005,7 +1005,7 @@
     half = jnp.bfloat16
     block = (rows, out_width)
     dma = pltpu.SemaphoreType.DMA
-    pieces = out_width // min(512, out_width)
+    pieces = out_width // min(1024, out_width)
     return pl.pallas_call(
         functools.partial(layer_kernel, far, near, peers, head_dim),
         out_shape=jax.ShapeDtypeStruct(block, half),

time: 90.6 us -> 89.3 us (0.986)
  Pallas kernels: 89.8 us -> 88.5 us
    pallas_call x1, Pallas kernels: 89.8 us -> 88.5 us  [fast_local(): pl.pallas_call(functools.partial(layer_kernel, far, near, peers, head_dim...]
where the time goes in v6:
time: 89.3 us; the launch traced here: 89.1 us
  Pallas kernels  88.5 us (99%)
    pallas_call x1, Pallas kernels, fast_local(): pl.pallas_call(functools.partial(layer_kernel, far, near, peers, head_dim...  88.5 us

profile of v6, /device:TPU:0, one launch (start us, length us, event | category | flops | bytes accessed | tf_op | source)
XLA Modules:
  0.0 89.1 jit_solution(14054689166531254640)
XLA Ops:
  0.0 88.5 %layer.1 = bf16[32,2048]{1,0:T(8,128)(2,1)S(1)} custom-call(s32[2,2]{1,0:T(2,128)} %refs_0_.1, bf16[128,3456]{1,0:T(8,128)(2,1)} %refs_1_.1, bf16[1152,1152]{1,0:T(8,128)(2,1)} %refs_2_.1, f32[36,128]{1,0:T(8,128)} %bitcast.9, f32[36,128]{1,0:T(8,128)} %bitcast.10, s32[6,32]{1,0:T(8,128)} %bitcast.11, bf16[8,2048]{1,0:T(8,128)(2,1)} %bitcast.8, ...), custom_call_target="tpu_custom_call" | custom-call | tf_op jit(solution)/shard_map/layer/pallas_call | solution.py:1009
  88.5 0.7 copy.13

commit v7 on v6

--- a/solution.py
+++ b/solution.py
@@ -301,7 +301,7 @@
             packed[peer, last : last + tail, :] = turned[
                 peer * tail : (peer + 1) * tail
             ].astype(jnp.bfloat16)
-    pl.semaphore_wait(barrier, devices - 1)
+    pl.semaphore_wait(barrier, peers)
     own_pair = pltpu.make_async_copy(pair_send.at[me], pair_recv.at[me], local_sem.at[1])
     own_value = pltpu.make_async_copy(value_send.at[me], value_recv.at[me], local_sem.at[4])
     own_pair.start()
@@ -926,7 +926,9 @@
     vision_scratch, language_scratch = scratch[:20], scratch[20:]
     place = lax.axis_index("wide")
     devices = lax.axis_size("wide")
-    barrier = greet([lax.rem(place + step, devices) for step in range(1, devices)])
+    start = place // peers * peers
+    clip_mates = [start + lax.rem(place - start + step, peers) for step in range(1, peers)]
+    barrier = greet(clip_mates + [lax.rem(place + peers, devices)])
     fetches = [
         pltpu.make_async_copy(source, target, small_sem.at[index])
         for index, (source, target) in enumerate(

time: 89.3 us -> 89.3 us (level)
  no operation moved by 1% of the time
where the time goes in v7:
time: 89.3 us; the launch traced here: 89.1 us
  Pallas kernels  88.5 us (99%)
    pallas_call x1, Pallas kernels, fast_local(): pl.pallas_call(functools.partial(layer_kernel, far, near, peers, head_dim...  88.5 us

profile of v7, /device:TPU:0, one launch (start us, length us, event | category | flops | bytes accessed | tf_op | source)
XLA Modules:
  0.0 89.1 jit_solution(8217349740082656233)
XLA Ops:
  0.0 88.5 %layer.1 = bf16[32,2048]{1,0:T(8,128)(2,1)S(1)} custom-call(s32[2,2]{1,0:T(2,128)} %refs_0_.1, bf16[128,3456]{1,0:T(8,128)(2,1)} %refs_1_.1, bf16[1152,1152]{1,0:T(8,128)(2,1)} %refs_2_.1, f32[36,128]{1,0:T(8,128)} %bitcast.9, f32[36,128]{1,0:T(8,128)} %bitcast.10, s32[6,32]{1,0:T(8,128)} %bitcast.11, bf16[8,2048]{1,0:T(8,128)(2,1)} %bitcast.8, ...), custom_call_target="tpu_custom_call" | custom-call | tf_op jit(solution)/shard_map/layer/pallas_call | solution.py:1011
  88.5 0.7 copy.13
